TPU v7x, 32 devices: a whole 2x2x4 slice. The times are simulated.
32 devices in a mesh: dp: 4 (over y, core), expert: 8 (over z, x).
Axes of the slice: x: 2, y: 2, z: 4, core: 2. Of those that a mesh axis runs over, the one named last changes fastest.
Arguments:
- patches: bfloat16 [16384, 768], P(('dp', 'expert')), may hold values from -6 to 6
- owner_slot: int32 [128], P(('dp', 'expert')), may hold values from 0 to 127, as said below
- segment_ids: int32 [16384], P(('dp', 'expert')), may hold values from 0 to 127, as said below
- block_mask: int32 [128, 4], P(('dp', 'expert')), may hold values from 0 to 1, as said below
- project_in: bfloat16 [768, 2304], replicated, may hold values from -30 to 30
- project_out: bfloat16 [768, 768], replicated, may hold values from -0.21875 to 0.21875
- slot_keys: bfloat16 [768, 32], replicated, may hold values from -30 to 30
- expert_in: bfloat16 [32, 768, 3072], P(('dp', 'expert')), may hold values from -0.21875 to 0.21875
- expert_out: bfloat16 [32, 3072, 768], P(('dp', 'expert')), may hold values from -0.109375 to 0.109375
Outputs:
- layer_out: bfloat16 [16384, 768], P(('dp', 'expert'))
Inputs may be any that keep to these rules, and one draw needn't show every extreme that they name: A permutation of the 128 blocks. Devices are numbered over dp then expert, and block g is read by device g // 4; it goes to device owner_slot[g] // 4, which has the same index along expert. Each reading device sends exactly 1 block to each of 4 distinct devices along dp, and each device receives exactly 4 blocks. `segment_ids`: Non-decreasing; the rows of run o (rows o * 512 to o * 512 + 511) carry the image numbers o * 4 to o * 4 + 3, each on one row or more. block_mask[o * 4 + a, b] is 1 when blocks a and b of run o hold rows of a common image, else 0.
All inputs are finite; a program needn't handle non-finite values.
Results may differ from a plain program's by a relative error of at most 0.0095.
The roundings to bfloat16 on the way count: a program that leaves them out, or rounds other values in their place, can miss the bound.
Values may be sent and summed in bfloat16 or wider, within the bound.
No kernel may reach another device: no remote copies, remote signals or barrier semaphores. Data moves between devices by JAX's collectives and lax.ppermute only.
A program may use at most 128 MiB of HBM per device.

v0:
```python
import jax
import jax.numpy as jnp
from jax import lax
from jax.sharding import PartitionSpec as P

HEADS = 12
HEAD = 64


EPS = 1e-06
NEGATIVE = -1e30


def layer_norm(values):
    values = values.astype(jnp.float32)
    centred = values - jnp.mean(values, axis=-1, keepdims=True)
    variance = jnp.mean(centred * centred, axis=-1, keepdims=True)
    return centred * lax.rsqrt(variance + EPS)


def per_device(
    patches,
    owner_slot,
    segment_ids,
    block_mask,
    project_in,
    project_out,
    slot_keys,
    expert_in,
    expert_out,
):
    width = patches.shape[1]
    blk_count = owner_slot.shape[0]
    tok_count = patches.shape[0]
    block_rows = tok_count // blk_count
    data_count = lax.axis_size("dp")
    column_count = lax.axis_size("expert")
    peer_cap = max(1, blk_count // data_count)
    slot_total = data_count * peer_cap
    highest = lax.Precision.HIGHEST
    target_data = owner_slot // blk_count // column_count
    target_place = owner_slot % blk_count
    to_peer = (target_data[:, None] == jnp.arange(data_count, dtype=jnp.int32)[None, :]).astype(
        jnp.int32
    )
    peer_rank = jnp.sum((jnp.cumsum(to_peer, axis=0) - 1) * to_peer, axis=1)
    send_index = target_data * peer_cap + peer_rank
    route = send_index[None, :] == jnp.arange(slot_total, dtype=jnp.int32)[:, None]
    flat_blocks = patches.reshape(blk_count, block_rows * width)
    send_rows = jnp.dot(
        route.astype(jnp.bfloat16), flat_blocks, preferred_element_type=jnp.float32
    ).astype(jnp.bfloat16)
    send_place = jnp.sum(route.astype(jnp.int32) * (target_place[None, :] + 1), axis=1) - 1
    arrived_rows, arrived_place = (
        lax.all_to_all(
            send_rows.reshape(data_count, peer_cap, block_rows * width),
            "dp",
            split_axis=0,
            concat_axis=0,
            tiled=True,
        ),
        lax.all_to_all(
            send_place.reshape(data_count, peer_cap), "dp", split_axis=0, concat_axis=0, tiled=True
        ),
    )
    placing = (
        arrived_place.reshape(1, slot_total) == jnp.arange(blk_count, dtype=jnp.int32)[:, None]
    ).astype(jnp.bfloat16)
    ordered = jnp.dot(
        placing,
        arrived_rows.reshape(slot_total, block_rows * width),
        preferred_element_type=jnp.float32,
    )
    ordered = ordered.astype(jnp.bfloat16).reshape(tok_count, width)
    normed = layer_norm(ordered).astype(jnp.bfloat16)
    joint = jnp.dot(normed, project_in, preferred_element_type=jnp.float32).astype(jnp.bfloat16)
    queries = joint[:, :width].reshape(tok_count, HEADS, HEAD)
    key_rows = joint[:, width : 2 * width].reshape(tok_count, HEADS, HEAD)
    value_rows = joint[:, 2 * width :].reshape(tok_count, HEADS, HEAD)
    linked_blocks = jnp.broadcast_to(
        block_mask[:, None, :, None] == 1, (blk_count, block_rows, blk_count, block_rows)
    ).reshape(tok_count, tok_count)
    linked = linked_blocks & (segment_ids[:, None] == segment_ids[None, :])
    scores = jnp.einsum(
        "qhd,khd->hqk", queries, key_rows, preferred_element_type=jnp.float32
    ) * HEAD ** (-0.5)
    scores = jnp.where(linked[None], scores, NEGATIVE)
    raised = jnp.exp(scores - jnp.max(scores, axis=2, keepdims=True))
    weights = (raised / jnp.sum(raised, axis=2, keepdims=True)).astype(jnp.bfloat16)
    attended = jnp.einsum("hqk,khd->qhd", weights, value_rows, preferred_element_type=jnp.float32)
    pieces = attended.astype(jnp.bfloat16).reshape(-1, width)
    hidden = (
        ordered.astype(jnp.float32)
        + jnp.dot(pieces, project_out, preferred_element_type=jnp.float32)
    ).astype(jnp.bfloat16)
    moe_normed = layer_norm(hidden).astype(jnp.bfloat16)
    logits = jnp.dot(moe_normed, slot_keys, preferred_element_type=jnp.float32)
    local_image = segment_ids % blk_count
    member = local_image[None, :] == jnp.arange(blk_count, dtype=jnp.int32)[:, None]
    member_float = member.astype(jnp.float32)
    column_max = jnp.max(jnp.where(member[:, :, None], logits[None], NEGATIVE), axis=1)
    row_shift = jnp.dot(member_float.T, column_max, precision=highest)
    raised_slots = jnp.exp(logits - row_shift)
    totals = jnp.dot(member_float, raised_slots, precision=highest)
    row_totals = jnp.dot(member_float.T, totals, precision=highest)
    dispatch = (raised_slots / row_totals).astype(jnp.bfloat16)
    masked = jnp.where(member[:, :, None], dispatch[None], jnp.zeros((), jnp.bfloat16))
    slot_in = jnp.einsum(
        "ste,td->sed", masked, moe_normed, preferred_element_type=jnp.float32
    ).astype(jnp.bfloat16)
    slot_raised = jnp.exp(logits - jnp.max(logits, axis=1, keepdims=True))
    combine = (slot_raised / jnp.sum(slot_raised, axis=1, keepdims=True)).astype(jnp.bfloat16)
    arrived = lax.all_to_all(slot_in, ("dp", "expert"), split_axis=1, concat_axis=0, tiled=True)
    inner = jnp.einsum("rkd,kdh->rkh", arrived, expert_in, preferred_element_type=jnp.float32)
    inner = jax.nn.gelu(inner, approximate=False).astype(jnp.bfloat16)
    produced = jnp.einsum(
        "rkh,khd->rkd", inner, expert_out, preferred_element_type=jnp.float32
    ).astype(jnp.bfloat16)
    returned = lax.all_to_all(produced, ("dp", "expert"), split_axis=0, concat_axis=1, tiled=True)
    masked_combine = jnp.where(member[:, :, None], combine[None], jnp.zeros((), jnp.bfloat16))
    mixture = jnp.einsum(
        "ste,sed->td", masked_combine, returned, preferred_element_type=jnp.float32
    )
    return (hidden.astype(jnp.float32) + mixture).astype(jnp.bfloat16)


def solution(mesh):
    in_specs = (
        P(("dp", "expert"), None),
        P(("dp", "expert")),
        P(("dp", "expert")),
        P(("dp", "expert"), None),
        P(),
        P(),
        P(),
        P(("dp", "expert"), None, None),
        P(("dp", "expert"), None, None),
    )
    out_specs = P(("dp", "expert"), None)
    return jax.shard_map(
        per_device, mesh=mesh, in_specs=in_specs, out_specs=out_specs, check_vma=False
    )
```

profile of v0, /device:TPU:0, one launch (start us, length us, event | category | flops | bytes accessed | tf_op | source)
XLA Modules:
  0.0 129.7 jit_solution(2665563277811735004)
XLA Ops:
  0.0 0.8 fusion.97
  0.9 0.2 select_reduce_fusion.2
  1.3 0.7 copy.42
  1.9 4.3 %all-to-all-start = ((s32[4,1,1]{2,1,0:T(1,128)}), s32[4,1,1]{2,1,0:T(1,128)S(1)}, u32[]{:S(2)}, u32[]{:S(2)}) async-start(s32[4,1,1]{2,1,0:T(1,128)} %copy.42), calls=%async_computation | async-start | bytes 4096 | tf_op jit(solution)/shard_map/all_to_all | solution.py:62
  6.2 2.6 %reshape.151 = bf16[4,98304]{1,0:T(4,128)(2,1)} reshape(bf16[512,768]{1,0:T(8,128)(2,1)} %param.9) | data formatting | bytes 1572864 | tf_op jit(solution)/shard_map/reshape | solution.py:49
  8.8 2.6 %fusion.2 = bf16[4,1,98304]{2,0,1:T(4,128)(2,1)} fusion(bf16[4,98304]{1,0:T(4,128)(2,1)} %reshape.151, s32[4]{0:T(128)S(1)} %add.54), kind=kOutput, calls=%fused_computation.4 | convolution fusion | flops 3538960 | bytes 1572880 | tf_op jit(solution)/shard_map/dot_general | solution.py:50
  11.4 0.5 broadcast.191
  11.9 3.6 %reduce.2 = bf16[4,98304]{1,0:T(4,128)(2,1)} reduce(bf16[4,1,98304]{2,0,1:T(4,128)(2,1)} %fusion.2, bf16[]{:T(256)} %broadcast.191), dimensions={1}, to_apply=%copy.43.reduce_sub_computation | reduce | bytes 1572866 | tf_op jit(solution)/shard_map/reshape | solution.py:56
  15.5 2.8 %reshape.168 = bf16[4,2,49152]{2,1,0:T(2,128)(2,1)} reshape(bf16[4,98304]{1,0:T(4,128)(2,1)} %reduce.2) | data formatting | bytes 1572864
  18.3 0.6 copy.45
  18.9 4.2 %all-to-all-start.1 = ((bf16[4,2,49152]{2,1,0:T(2,128)(2,1)}), bf16[4,2,49152]{2,1,0:T(2,128)(2,1)}, u32[]{:S(2)}, u32[]{:S(2)}) async-start(bf16[4,2,49152]{2,1,0:T(2,128)(2,1)} %reshape.168), calls=%async_computation.1 | async-start | bytes 1572864 | tf_op jit(solution)/shard_map/all_to_all | solution.py:55
  23.1 0.9 broadcast_in_dim.61
  24.0 1.0 bitcast_and_fusion
  25.1 9.6 %all-to-all-done.1 = bf16[4,2,49152]{2,1,0:T(2,128)(2,1)} async-done(((bf16[4,2,49152]{2,1,0:T(2,128)(2,1)}), bf16[4,2,49152]{2,1,0:T(2,128)(2,1)}, u32[]{:S(2)}, u32[]{:S(2)}) %all-to-all-start.1) | async-done | bytes 786464 | tf_op jit(solution)/shard_map/all_to_all | solution.py:55
  34.8 3.7 %reshape.169 = bf16[4,1,98304]{2,1,0:T(2,128)(2,1)} reshape(bf16[4,2,49152]{2,1,0:T(2,128)(2,1)} %all-to-all-done.1) | data formatting | bytes 1572864
  38.5 3.6 %fusion.1 = f32[4,98304]{1,0:T(4,128)} fusion(bf16[4,1,98304]{2,1,0:T(2,128)(2,1)} %reshape.169, s32[4]{0:T(128)S(1)} %reduce), kind=kOutput, calls=%fused_computation.3 | convolution fusion | flops 3932176 | bytes 2359312 | tf_op jit(solution)/shard_map/dot_general | solution.py:69
  42.2 3.7 %reshape.163 = f32[512,768]{1,0:T(8,128)} reshape(f32[4,98304]{1,0:T(4,128)} %fusion.1) | data formatting | bytes 3145728 | tf_op jit(solution)/shard_map/convert_element_type | solution.py:93
  45.8 1.6 %reduce_sum.74 = f32[512]{0:T(512)S(1)} reduce(f32[512,768]{1,0:T(8,128)} %reshape.163, f32[]{:T(128)} %constant.50.clone.1), dimensions={1}, to_apply=%region_3.4 | reduce | flops 392704 | bytes 1574916 | tf_op jit(solution)/shard_map/reduce_sum | solution.py:16
  47.4 1.8 %multiply_reduce_fusion = f32[512]{0:T(512)S(1)} fusion(f32[512,768]{1,0:T(8,128)} %reshape.163, f32[512]{0:T(512)S(1)} %broadcast_multiply_fusion.1), kind=kLoop, calls=%fused_computation.46 | loop fusion | flops 1179136 | bytes 1576960 | tf_op jit(solution)/shard_map/reduce_sum | solution.py:17
  49.3 2.1 %convolution_convert_fusion.2 = bf16[512,2304]{1,0:T(8,128)(2,1)S(1)} fusion(bf16[768,2304]{1,0:T(8,128)(2,1)S(1)} %copy-done, f32[512,768]{1,0:T(8,128)S(1)} %copy-done.1, f32[512]{0:T(512)S(1)} %add_rsqrt_fusion.1, f32[512]{0:T(512)S(1)} %broadcast_multiply_fusion.1), kind=kOutput, calls=%fused_computation.17 | convolution fusion | flops 1814298624 | bytes 7475200 | tf_op jit(solution)/shard_map/dot_general | solution.py:76
  51.4 1.5 %fusion.133 = (bf16[512,768]{1,0:T(8,128)(2,1)}, bf16[512,768]{1,0:T(8,128)(2,1)}, bf16[512,768]{1,0:T(8,128)(2,1)}) fusion(bf16[512,2304]{1,0:T(8,128)(2,1)S(1)} %convolution_convert_fusion.2), kind=kLoop, calls=%fused_computation.172 | loop fusion | bytes 4718592 | tf_op jit(solution)/shard_map/slice | solution.py:78
  52.8 2.3 %copy.44 = bf16[512,768]{0,1:T(8,128)(2,1)} copy(bf16[512,768]{1,0:T(8,128)(2,1)} %get-tuple-element.7) | data formatting | bytes 1572864 | tf_op jit(solution)/shard_map/slice | solution.py:79
  55.1 2.3 %copy.46 = bf16[512,768]{0,1:T(8,128)(2,1)} copy(bf16[512,768]{1,0:T(8,128)(2,1)} %get-tuple-element.6) | data formatting | bytes 1572864 | tf_op jit(solution)/shard_map/slice | solution.py:77
  57.4 2.3 %copy.47 = bf16[512,768]{0,1:T(8,128)(2,1)} copy(bf16[512,768]{1,0:T(8,128)(2,1)} %get-tuple-element.5) | data formatting | bytes 1572864 | tf_op jit(solution)/shard_map/slice | solution.py:78
  59.7 11.2 %fusion.134 = (f32[12,512]{1,0:T(8,128)}, f32[12,512,512]{1,2,0:T(8,128)}) fusion(pred[512,512]{0,1:T(8,128)(4,1)} %bitcast_and_fusion, bf16[512,12,64]{0,2,1:T(8,128)(2,1)} %bitcast.139, bf16[512,12,64]{0,2,1:T(8,128)(2,1)} %bitcast.140), kind=kOutput, calls=%fused_computation.173 | convolution fusion | flops 415236608 | bytes 14442496 | tf_op jit(solution)/shard_map/sub | solution.py:88
  70.9 6.1 %fusion.31 = bf16[12,64,512]{2,1,0:T(8,128)(2,1)S(1)} fusion(bf16[512,12,64]{0,2,1:T(8,128)(2,1)} %bitcast.138, f32[12,512,512]{1,2,0:T(8,128)} %get-tuple-element.11, f32[12,512]{1,0:T(8,128)} %get-tuple-element.10), kind=kOutput, calls=%fused_computation.49 | convolution fusion | flops 409337856 | bytes 14180352 | tf_op jit(solution)/shard_map/hqk,khd->qhd/dot_general | solution.py:90
  77.0 0.9 convert_reduce_fusion
  78.0 0.4 fusion.14
  78.4 0.3 fusion.15
  78.6 0.2 copy-done.5
  78.8 0.3 fusion.135
  79.3 0.2 fusion.40
  79.7 0.3 fusion.41
  79.9 0.3 convolution_convert_fusion.3
  80.2 0.4 copy.49
  80.6 13.5 %all_to_all.44 = bf16[4,32,768]{2,0,1:T(4,128)(2,1)} all-to-all(bf16[4,32,768]{2,0,1:T(4,128)(2,1)S(1)} %copy.49), channel_id=1, replica_groups=mesh['dp'=4,'expert'=8] {'dp','expert'}, dimensions={1} | all-to-all | bytes 393216 | tf_op jit(solution)/shard_map/all_to_all | solution.py:113
  94.1 1.7 %reshape.159 = bf16[128,768]{1,0:T(8,128)(2,1)} reshape(bf16[32,4,1,768]{3,1,0,2:T(4,128)(2,1)} %bitcast.141) | data formatting | bytes 393216 | tf_op jit(solution)/shard_map/reshape.1
  95.8 9.2 %fusion.37 = bf16[128,1,768]{2,0,1:T(8,128)(2,1)} fusion(bf16[1,3072,768]{2,1,0:T(8,128)(2,1)} %param.17, bf16[128,768]{1,0:T(8,128)(2,1)} %reshape.159, bf16[1,768,3072]{2,1,0:T(8,128)(2,1)} %param.16), kind=kOutput, calls=%fused_computation.53 | convolution fusion | flops 1233616896 | bytes 9830400 | tf_op jit(solution)/shard_map/rkh,khd->rkd/dot_general | solution.py:116
  104.9 2.2 %reduce.3 = bf16[128,768]{1,0:T(8,128)(2,1)} reduce(bf16[128,1,768]{2,0,1:T(8,128)(2,1)} %fusion.37, bf16[]{:T(256)} %broadcast.191), dimensions={1}, to_apply=%copy.50.reduce_sub_computation | reduce | bytes 393218 | tf_op jit(solution)/shard_map/convert_element_type | solution.py:118
  107.2 1.7 %reshape.170 = bf16[32,2,1536]{2,1,0:T(2,128)(2,1)} reshape(bf16[128,768]{1,0:T(8,128)(2,1)} %reduce.3) | data formatting | bytes 393216
  108.9 3.4 %all-to-all-start.3 = ((bf16[32,2,1536]{2,1,0:T(2,128)(2,1)}), bf16[32,2,1536]{2,1,0:T(2,128)(2,1)}, u32[]{:S(2)}, u32[]{:S(2)}) async-start(bf16[32,2,1536]{2,1,0:T(2,128)(2,1)} %reshape.170), calls=%async_computation.3 | async-start | bytes 393216 | tf_op jit(solution)/shard_map/all_to_all | solution.py:119
  112.3 0.9 fusion.92
  113.2 1.5 %divide_convert_fusion.4 = bf16[512,32]{0,1:T(8,128)(2,1)} fusion(f32[512,32]{0,1:T(8,128)} %copy-done.4, f32[512]{0:T(512)S(1)} %fusion.92, f32[512]{0:T(512)S(1)} %get-tuple-element.14), kind=kLoop, calls=%fused_computation.105 | loop fusion | flops 49152 | bytes 102400 | tf_op jit(solution)/shard_map/convert_element_type | solution.py:112
  114.6 5.9 %all-to-all-done.3 = bf16[32,2,1536]{2,1,0:T(2,128)(2,1)} async-done(((bf16[32,2,1536]{2,1,0:T(2,128)(2,1)}), bf16[32,2,1536]{2,1,0:T(2,128)(2,1)}, u32[]{:S(2)}, u32[]{:S(2)}) %all-to-all-start.3) | async-done | bytes 196640 | tf_op jit(solution)/shard_map/all_to_all | solution.py:119
  120.6 2.2 %reshape.171 = bf16[128,1,768]{2,1,0:T(2,128)(2,1)} reshape(bf16[32,2,1536]{2,1,0:T(2,128)(2,1)} %all-to-all-done.3) | data formatting | bytes 393216
  122.8 2.7 %reduce.1 = bf16[128,768]{1,0:T(8,128)(2,1)} reduce(bf16[128,1,768]{2,1,0:T(2,128)(2,1)} %reshape.171, bf16[]{:T(256)} %constant.140), dimensions={1}, to_apply=%all_to_all.36.reduce_sub_computation | reduce | bytes 393218 | tf_op jit(solution)/shard_map/all_to_all | solution.py:119
  125.5 1.6 %all_to_all.37 = bf16[32,4,1,768]{3,1,0,2:T(4,128)(2,1)} reshape(bf16[128,768]{1,0:T(8,128)(2,1)} %reduce.1) | data formatting | bytes 393216 | tf_op jit(solution)/shard_map/all_to_all | solution.py:119
  127.2 2.5 %fusion.16 = bf16[512,768]{1,0:T(8,128)(2,1)} fusion(bf16[512,768]{1,0:T(8,128)(2,1)} %copy-done.3, bf16[32,4,1,768]{3,1,0,2:T(4,128)(2,1)} %all_to_all.37, pred[4,512]{1,0:T(4,128)(4,1)S(1)} %iota_compare_fusion, bf16[512,32]{0,1:T(8,128)(2,1)} %divide_convert_fusion.4), kind=kOutput, calls=%fused_computation.26 | convolution fusion | flops 101908480 | bytes 1804288 | tf_op jit(solution)/shard_map/ste,sed->td/dot_general | solution.py:121
  (33 shorter events, 0.7 us)
Async XLA Ops:
  0.0 49.3 %copy-start = (bf16[768,2304]{1,0:T(8,128)(2,1)S(1)}, bf16[768,2304]{1,0:T(8,128)(2,1)}, u32[]{:S(2)}) copy-start(bf16[768,2304]{1,0:T(8,128)(2,1)} %param.13) | copy-start | bytes 10616836
  1.9 17.0 %all-to-all-start = ((s32[4,1,1]{2,1,0:T(1,128)}), s32[4,1,1]{2,1,0:T(1,128)S(1)}, u32[]{:S(2)}, u32[]{:S(2)}) async-start(s32[4,1,1]{2,1,0:T(1,128)} %copy.42), calls=%async_computation | async-start | bytes 4096 | tf_op jit(solution)/shard_map/all_to_all | solution.py:62
  11.9 6.4 %copy-start.7 = (s32[4,4]{1,0:T(4,128)S(1)}, s32[4,4]{1,0:T(4,128)}, u32[]{:S(2)}) copy-start(s32[4,4]{1,0:T(4,128)} %param.12) | copy-start | bytes 196
  15.4 7.6 %copy-start.6 = (s32[512]{0:T(512)S(1)}, s32[512]{0:T(512)}, u32[]{:S(2)}) copy-start(s32[512]{0:T(512)} %param.11) | copy-start | bytes 6148
  18.9 15.9 %all-to-all-start.1 = ((bf16[4,2,49152]{2,1,0:T(2,128)(2,1)}), bf16[4,2,49152]{2,1,0:T(2,128)(2,1)}, u32[]{:S(2)}, u32[]{:S(2)}) async-start(bf16[4,2,49152]{2,1,0:T(2,128)(2,1)} %reshape.168), calls=%async_computation.1 | async-start | bytes 1572864 | tf_op jit(solution)/shard_map/all_to_all | solution.py:55
  47.4 1.9 %copy-start.1 = (f32[512,768]{1,0:T(8,128)S(1)}, f32[512,768]{1,0:T(8,128)}, u32[]{:S(2)}) copy-start(f32[512,768]{1,0:T(8,128)} %reshape.163) | copy-start | bytes 4718596
  70.9 6.1 %copy-start.2 = (f32[512,768]{1,0:T(8,128)S(1)}, f32[512,768]{1,0:T(8,128)}, u32[]{:S(2)}) copy-start(f32[512,768]{1,0:T(8,128)} %reshape.163) | copy-start | bytes 4718596
  70.9 6.1 %copy-start.8 = (bf16[768,768]{1,0:T(8,128)(2,1)S(1)}, bf16[768,768]{1,0:T(8,128)(2,1)}, u32[]{:S(2)}) copy-start(bf16[768,768]{1,0:T(8,128)(2,1)} %param.14) | copy-start | bytes 3538948
  78.0 1.2 copy-start.3
  78.0 0.8 copy-start.5
  79.2 1.0 copy-start.4
  108.9 11.7 %all-to-all-start.3 = ((bf16[32,2,1536]{2,1,0:T(2,128)(2,1)}), bf16[32,2,1536]{2,1,0:T(2,128)(2,1)}, u32[]{:S(2)}, u32[]{:S(2)}) async-start(bf16[32,2,1536]{2,1,0:T(2,128)(2,1)} %reshape.170), calls=%async_computation.3 | async-start | bytes 393216 | tf_op jit(solution)/shard_map/all_to_all | solution.py:119
where the time goes:
time: 131 us; the launch traced here: 130 us
  matrix products  39.4 us (30%)
  local copies, waits for them, and re-layouts  31.7 us (24%)
  other arithmetic  17.4 us (13%)
  waiting for transfers between devices  15.6 us (12%)
  blocking collectives  13.5 us (10%)
  starting transfers between devices  11.9 us (9%)
    all_to_all x1, blocking collectives, per_device(): lax.all_to_all(slot_in, ('dp', 'expert'), split_axis=1, concat_axis=0, ti...  13.5 us
    sub x1, matrix products, per_device(): raised = jnp.exp(scores - jnp.max(scores, axis=2, keepdims=True))  11.2 us
    unnamed x22, local copies, waits for them, and re-layouts  10.7 us
    all_to_all x1, waiting for transfers between devices, per_device(): lax.all_to_all(send_rows.reshape(data_count, peer_cap, block_rows * width...  9.65 us
    dot_general x1, matrix products, per_device(): jnp.einsum('rkh,khd->rkd', inner, expert_out, preferred_element_type=jnp....  9.17 us
    dot_general x1, matrix products, per_device(): jnp.einsum('hqk,khd->qhd', weights, value_rows, preferred_element_type=jn...  6.08 us
    all_to_all x1, waiting for transfers between devices, per_device(): lax.all_to_all(produced, ('dp', 'expert'), split_axis=0, concat_axis=1, t...  5.92 us
    all_to_all x1, starting transfers between devices, per_device(): lax.all_to_all(send_place.reshape(data_count, peer_cap), 'dp', split_axis...  4.26 us
  transfers between devices with their start and end apart: 3, of which 2 were waited for; matrix products, arithmetic and copies ran while one was open for 13% of the time, Pallas kernels for 0%

commit v1 on v0

v1 whole, which is shorter than its diff:
```python
import functools
import math

import jax
import jax.numpy as jnp
from jax import lax
from jax.experimental import pallas as pl
from jax.experimental.pallas import tpu as pltpu
from jax.sharding import PartitionSpec as P

HEAD = 64
LANES = 128
TAG_ROWS = 8
EPS = 1e-06
NEGATIVE = -1e30
AXES = ("dp", "expert")


def layer_norm(values):
    centred = values - jnp.mean(values, axis=-1, keepdims=True)
    variance = jnp.mean(centred * centred, axis=-1, keepdims=True)
    return centred * lax.rsqrt(variance + EPS)


def dot(a, b, dims=((1,), (0,))):
    return lax.dot_general(a, b, (dims, ((), ())), preferred_element_type=jnp.float32)


def front_kernel(
    self_ref,
    patches_ref,
    *refs,
    slots,
):
    arrived = refs[:slots]
    (
        query_mark_ref,
        key_mark_ref,
        member_ref,
        project_in_ref,
        project_out_ref,
        slot_keys_ref,
        hidden_ref,
        slot_in_ref,
        combine_ref,
        ordered_ref,
        joint_ref,
        context_ref,
    ) = refs[slots:]
    tok_count, width = ordered_ref.shape
    rows = arrived[0].shape[0] - TAG_ROWS

    def place_block(block, place):
        at = pl.ds(pl.multiple_of(place * rows, rows), rows)
        ordered_ref[at, :] = block
        normed = layer_norm(block.astype(jnp.float32)).astype(jnp.bfloat16)
        joint_ref[at, :] = dot(normed, project_in_ref[...]).astype(jnp.bfloat16)

    place_block(
        patches_ref[pl.ds(pl.multiple_of(self_ref[0] * rows, rows), rows), :], self_ref[1]
    )
    for ref in arrived:
        tag = jnp.max(ref[rows:, :LANES].astype(jnp.float32)).astype(jnp.int32)

        @pl.when(tag >= 0)
        def _():
            place_block(ref[:rows, :], tag)

    lane = lax.broadcasted_iota(jnp.int32, (1, LANES), 1)
    first = lane < HEAD
    ones = jnp.ones((tok_count, LANES), jnp.bfloat16)
    zero = jnp.zeros((), jnp.bfloat16)
    scale = HEAD ** (-0.5) * math.log2(math.e)
    for pair in range(width // LANES):
        at = pair * LANES
        query = joint_ref[:, at : at + LANES]
        key = joint_ref[:, width + at : width + at + LANES]
        value = joint_ref[:, 2 * width + at : 2 * width + at + LANES]
        keys = jnp.concatenate([key, key_mark_ref[...]], axis=1)
        values = jnp.concatenate([value, ones], axis=1)
        parts = []
        for keep in (first, ~first):
            queries = jnp.concatenate(
                [jnp.where(keep, query, zero), query_mark_ref[...]], axis=1
            )
            scores = dot(queries, keys, ((1,), (1,)))
            top = jnp.max(scores, axis=1, keepdims=True)
            raised = jnp.exp2((scores - top) * scale).astype(jnp.bfloat16)
            parts.append(dot(raised, values))
        picked = jnp.where(first, parts[0][:, :LANES], parts[1][:, :LANES])
        total = jnp.where(first, parts[0][:, LANES:], parts[1][:, LANES:])
        context_ref[:, at : at + LANES] = (picked / total).astype(jnp.bfloat16)

    hidden = (
        ordered_ref[...].astype(jnp.float32) + dot(context_ref[...], project_out_ref[...])
    ).astype(jnp.bfloat16)
    hidden_ref[...] = hidden
    moe_normed = layer_norm(hidden.astype(jnp.float32)).astype(jnp.bfloat16)
    logits = dot(moe_normed, slot_keys_ref[...])
    member = member_ref[...] > 0
    column_top = jnp.max(jnp.where(member, logits, NEGATIVE), axis=0, keepdims=True)
    column_raised = jnp.where(member, jnp.exp(logits - column_top), 0.0)
    dispatch = column_raised / jnp.sum(column_raised, axis=0, keepdims=True)
    slot_in = dot(dispatch.astype(jnp.bfloat16), moe_normed, ((0,), (0,)))
    slot_in_ref[...] = slot_in.astype(jnp.bfloat16).reshape(slot_in_ref.shape)
    row_top = jnp.max(logits, axis=1, keepdims=True)
    row_raised = jnp.where(member, jnp.exp(logits - row_top), 0.0)
    combine = row_raised / jnp.sum(row_raised, axis=1, keepdims=True)
    combine_ref[...] = combine.astype(jnp.bfloat16)


def expert_kernel(arrived_ref, expert_in_ref, expert_out_ref, produced_ref, total_ref):
    step = pl.program_id(0)
    rows = total_ref.shape[0]
    slots = arrived_ref[...].reshape(rows, total_ref.shape[1])
    inner = dot(slots, expert_in_ref[...])
    inner = 0.5 * inner * (1.0 + lax.erf(inner * math.sqrt(0.5)))
    part = dot(inner.astype(jnp.bfloat16), expert_out_ref[...])

    @pl.when(step == 0)
    def _():
        total_ref[...] = part

    @pl.when(step > 0)
    def _():
        total_ref[...] += part

    @pl.when(step == pl.num_programs(0) - 1)
    def _():
        produced_ref[...] = total_ref[...].astype(jnp.bfloat16).reshape(produced_ref.shape)


def combine_kernel(hidden_ref, combine_ref, returned_ref, out_ref):
    returned = returned_ref[...].reshape(combine_ref.shape[1], hidden_ref.shape[1])
    mixture = dot(combine_ref[...], returned)
    out_ref[...] = (hidden_ref[...].astype(jnp.float32) + mixture).astype(jnp.bfloat16)


def whole(memory_space=pltpu.VMEM):
    return pl.BlockSpec(memory_space=memory_space)


def per_device(
    patches,
    owner_slot,
    segment_ids,
    block_mask,
    project_in,
    project_out,
    slot_keys,
    expert_in,
    expert_out,
):
    tok_count, width = patches.shape
    blk_count = owner_slot.shape[0]
    rows = tok_count // blk_count
    data_count = lax.axis_size("dp")
    column_count = lax.axis_size("expert")
    expert_count = slot_keys.shape[1]
    hidden_width = expert_in.shape[2]
    me = lax.axis_index("dp")

    target_data = owner_slot // blk_count // column_count
    target_place = owner_slot % blk_count
    block_index = jnp.arange(blk_count, dtype=jnp.int32)

    def route(flip):
        chosen = target_data == me ^ flip
        source = jnp.sum(jnp.where(chosen, block_index, 0))
        place = jnp.sum(jnp.where(chosen, target_place + 1, 0)) - 1
        return source, place

    arrived = []
    for flip in [*range(2, data_count), 1]:
        source, place = route(flip)
        block = lax.dynamic_slice(patches, (source * rows, 0), (rows, width))
        tag = jnp.full((TAG_ROWS, width), place.astype(jnp.bfloat16))
        arrived.append(
            lax.ppermute(
                jnp.concatenate([block, tag], axis=0),
                "dp",
                [(i, i ^ flip) for i in range(data_count)],
            )
        )
    self_info = jnp.stack(route(0))

    local_image = segment_ids % blk_count
    block_of = jnp.arange(tok_count, dtype=jnp.int32) // rows
    column = jnp.arange(LANES, dtype=jnp.int32)[None, :]
    image_is = local_image[:, None] == column
    block_is = block_of[:, None] == column - blk_count
    unlinked = jnp.repeat(block_mask != 1, rows, axis=0)
    blocked = jnp.pad(unlinked, ((0, 0), (blk_count, LANES - 2 * blk_count)))
    query_mark = jnp.where(image_is | blocked, NEGATIVE, 0.0).astype(jnp.bfloat16)
    key_mark = (jnp.where(column < blk_count, ~image_is, block_is)).astype(jnp.bfloat16)
    columns = expert_count * blk_count
    column_image = jnp.arange(columns, dtype=jnp.int32)[None, :] % blk_count
    member = (local_image[:, None] == column_image).astype(jnp.float32)
    slot_keys_wide = jnp.repeat(slot_keys, blk_count, axis=1)

    hidden, slot_in, combine = pl.pallas_call(
        functools.partial(front_kernel, slots=len(arrived)),
        out_shape=(
            jax.ShapeDtypeStruct((tok_count, width), jnp.bfloat16),
            jax.ShapeDtypeStruct((expert_count, blk_count, width), jnp.bfloat16),
            jax.ShapeDtypeStruct((tok_count, columns), jnp.bfloat16),
        ),
        in_specs=[whole(pltpu.SMEM)] + [whole()] * (7 + len(arrived)),
        out_specs=(whole(),) * 3,
        scratch_shapes=[
            pltpu.VMEM((tok_count, width), jnp.bfloat16),
            pltpu.VMEM((tok_count, 3 * width), jnp.bfloat16),
            pltpu.VMEM((tok_count, width), jnp.bfloat16),
        ],
        name="front",
    )(
        self_info,
        patches,
        *arrived,
        query_mark,
        key_mark,
        member,
        project_in,
        project_out,
        slot_keys_wide,
    )
    slots_here = lax.all_to_all(slot_in, AXES, split_axis=0, concat_axis=0, tiled=True)
    step = min(hidden_width, 768)
    row_count = expert_count * blk_count
    produced = pl.pallas_call(
        expert_kernel,
        out_shape=jax.ShapeDtypeStruct(slots_here.shape, jnp.bfloat16),
        grid=(hidden_width // step,),
        in_specs=[
            pl.BlockSpec(slots_here.shape, lambda i: (0, 0, 0)),
            pl.BlockSpec((None, width, step), lambda i: (0, 0, i)),
            pl.BlockSpec((None, step, width), lambda i: (0, i, 0)),
        ],
        out_specs=pl.BlockSpec(slots_here.shape, lambda i: (0, 0, 0)),
        scratch_shapes=[pltpu.VMEM((row_count, width), jnp.float32)],
        name="expert",
    )(slots_here, expert_in, expert_out)
    returned = lax.all_to_all(produced, AXES, split_axis=0, concat_axis=0, tiled=True)
    return pl.pallas_call(
        combine_kernel,
        out_shape=jax.ShapeDtypeStruct((tok_count, width), jnp.bfloat16),
        in_specs=[whole()] * 3,
        out_specs=whole(),
        name="combine",
    )(hidden, combine, returned)


def solution(mesh):
    in_specs = (
        P(AXES, None),
        P(AXES),
        P(AXES),
        P(AXES, None),
        P(),
        P(),
        P(),
        P(AXES, None, None),
        P(AXES, None, None),
    )
    return jax.shard_map(
        per_device, mesh=mesh, in_specs=in_specs, out_specs=P(AXES, None), check_vma=False
    )
```

time: 131 us -> 66.4 us (0.51)
  matrix products: 39.4 us -> 0 us
  local copies, waits for them, and re-layouts: 31.7 us -> 3.71 us
  Pallas kernels: 0 us -> 21.8 us
  waiting for transfers between devices: 15.6 us -> 0.36 us
  blocking collectives: 13.5 us -> 26.3 us
  other arithmetic: 17.4 us -> 5.97 us
  starting transfers between devices: 11.9 us -> 3.31 us
  between operations: 0.22 us -> 4.49 us
    dot_general x12 -> x0, matrix products: 28.2 us -> none  [the longest x1 9.17 us: per_device(): jnp.einsum('rkh,khd->rkd', inner, expert_out, preferred_element_type=jnp....]
    pallas_call x0 -> x3, Pallas kernels: none -> 21.8 us  [the longest x1 13.1 us: per_device(): pl.pallas_call(functools.partial(front_kernel, slots=len(arrived)), out_s...]
    all_to_all x3 -> x0, waiting for transfers between devices: 15.6 us -> none  [the longest x1 9.65 us: per_device(): lax.all_to_all(send_rows.reshape(data_count, peer_cap, block_rows * width...]
    all_to_all x1 -> x2, blocking collectives: 13.5 us -> 26.3 us  [the longest x1 14.6 us: per_device(): lax.all_to_all(slot_in, AXES, split_axis=0, concat_axis=0, tiled=True)]
    all_to_all x3 -> x0, starting transfers between devices: 11.9 us -> none  [the longest x1 4.26 us: per_device(): lax.all_to_all(send_place.reshape(data_count, peer_cap), 'dp', split_axis...]
    sub x1 -> x0, matrix products: 11.2 us -> none  [per_device(): raised = jnp.exp(scores - jnp.max(scores, axis=2, keepdims=True))]
    unnamed x22 -> x6, local copies, waits for them, and re-layouts: 10.7 us -> 0.76 us
    slice x4 -> x0, local copies, waits for them, and re-layouts: 8.38 us -> none  [the longest x2 3.79 us: per_device(): key_rows = joint[:, width:2 * width].reshape(tok_count, HEADS, HEAD)]
  transfers between devices with their start and end apart: 3 -> 3, of which waited for: 2 -> 1; matrix products, arithmetic and copies ran while one was open for 13% -> 9% of each run, Pallas kernels for 0% -> 0%
where the time goes in v1:
time: 66.4 us; the launch traced here: 65.9 us
  blocking collectives  26.3 us (40%)
  Pallas kernels  21.8 us (33%)
  other arithmetic  5.97 us (9%)
  between operations  4.49 us (7%)
  local copies, waits for them, and re-layouts  3.71 us (6%)
  starting transfers between devices  3.31 us (5%)
    all_to_all x1, blocking collectives, per_device(): lax.all_to_all(slot_in, AXES, split_axis=0, concat_axis=0, tiled=True)  14.6 us
    pallas_call x1, Pallas kernels, per_device(): pl.pallas_call(functools.partial(front_kernel, slots=len(arrived)), out_s...  13.1 us
    all_to_all x1, blocking collectives, per_device(): lax.all_to_all(produced, AXES, split_axis=0, concat_axis=0, tiled=True)  11.7 us
    pallas_call x1, Pallas kernels, per_device(): pl.pallas_call(expert_kernel, out_shape=jax.ShapeDtypeStruct(slots_here.s...  6.25 us
    ppermute x3, starting transfers between devices, per_device(): lax.ppermute(jnp.concatenate([block, tag], axis=0), 'dp', [(i, i ^ flip)...  3.31 us
    pallas_call x1, Pallas kernels, per_device(): pl.pallas_call(combine_kernel, out_shape=jax.ShapeDtypeStruct((tok_count,...  2.47 us
  transfers between devices with their start and end apart: 3, of which 1 were waited for; matrix products, arithmetic and copies ran while one was open for 9% of the time, Pallas kernels for 0%

profile of v1, /device:TPU:0, one launch (start us, length us, event | category | flops | bytes accessed | tf_op | source)
XLA Modules:
  0.0 65.9 jit_solution(14129250162480615891)
XLA Ops:
  0.0 0.7 %and_select_fusion.2 = (s32[4]{0:T(128)S(1)}, s32[4]{0:T(128)S(1)}) fusion(s32[4]{0:T(128)} %param.10), kind=kLoop, calls=%fused_computation.20 | loop fusion | flops 140 | bytes 48 | tf_op jit(solution)/shard_map/jit(floor_divide)/jit(_where)/select_n | solution.py:163
  0.7 0.8 %fusion.15 = (s32[]{:T(128)}, s32[]{:T(128)}, s32[]{:T(128)}, s32[]{:T(128)}, s32[]{:T(128)}, /*index=5*/s32[]{:T(128)}, s32[]{:T(128)}, s32[]{:T(128)}) fusion(s32[4]{0:T(128)S(1)} %get-tuple-element.25, s32[4]{0:T(128)S(1)} %get-tuple-element.24, s32[]{:T(128)S(6)} %xor.11, s32[]{:T(128)S(6)} %xor.10, s32[]{:T(128)S(6)} %xor.9, s32[]{:T(128)S(6)} %axis_index.15), kind=kLoop, calls=%fused_computation.47 | loop fusion | flops 72 | bytes 80 | tf_op jit(solution)/shard_map/reduce_sum | solution.py:170
  3.9 1.2 %constant_dynamic-slice_fusion = (bf16[128,768]{1,0:T(8,128)(2,1)S(1)}, bf16[128,768]{1,0:T(8,128)(2,1)S(1)}, bf16[128,768]{1,0:T(8,128)(2,1)S(1)}) fusion(bf16[512,768]{1,0:T(8,128)(2,1)} %patches_ref.1, s32[]{:T(128)S(6)} %select_n.95, s32[]{:T(128)S(6)} %select_n.92, s32[]{:T(128)S(6)} %select_n.89), kind=kLoop, calls=%fused_computation.37 | loop fusion | bytes 1179660 | tf_op jit(solution)/shard_map/dynamic_slice | solution.py:176
  5.1 3.1 %collective-permute-start = (bf16[136,768]{1,0:T(8,128)(2,1)S(1)}, bf16[136,768]{1,0:T(8,128)(2,1)S(1)}, u32[]{:S(2)}, u32[]{:S(2)}) collective-permute-start(bf16[136,768]{1,0:T(8,128)(2,1)S(1)} %concatenate.9), channel_id=1, source_target_pairs={{0,16},{8,24},{16,0},{24,8},{1,17},{9,25},{17,1},{25,9},{2,18},{10... | collective-permute-start | bytes 626696 | tf_op jit(solution)/shard_map/ppermute | solution.py:179
  8.9 0.1 collective-permute-start.1
  9.7 0.2 collective-permute-start.2
  9.8 0.7 %broadcast_compare_fusion = pred[4,4]{1,0:T(4,128)(4,1)S(1)} fusion(s32[4,4]{1,0:T(4,128)} %param.12), kind=kLoop, calls=%fused_computation.36 | loop fusion | flops 16 | bytes 80 | tf_op jit(solution)/shard_map/ne | solution.py:192
  11.2 0.7 %add_select_fusion.1 = s32[512]{0:T(512)S(1)} fusion(s32[512]{0:T(512)} %param.11), kind=kLoop, calls=%fused_computation.11 | loop fusion | flops 5632 | bytes 4096 | tf_op jit(solution)/shard_map/jit(remainder)/select_n | solution.py:187
  11.9 0.9 %broadcast_in_dim.43 = bf16[768,32,4]{0,2,1:T(4,128)(2,1)S(1)} broadcast(bf16[768,32]{0,1:T(8,128)(2,1)} %param.15), dimensions={0,1} | broadcast | bytes 245760 | tf_op jit(solution)/shard_map/broadcast_in_dim | solution.py:199
  12.7 0.1 reshape.46
  12.8 0.8 %copy.11.refs_8_ = bf16[768,128]{1,0:T(8,128)(2,1)} copy(bf16[768,128]{0,1:T(8,128)(2,1)S(1)} %reshape.46) | data formatting | bytes 393216 | tf_op jit(solution)/shard_map/reshape | solution.py:199
  13.6 1.3 %pad_add_fusion.self_ref = s32[2]{0:T(128)} fusion(s32[1]{0:T(128)} %bitcast.1, s32[1]{0:T(128)} %bitcast), kind=kLoop, calls=%fused_computation.49 | loop fusion | flops 2 | bytes 16 | tf_op jit(solution)/shard_map/stack | solution.py:185
  14.9 0.9 %compare_convert_fusion = (f32[512,128]{1,0:T(8,128)}, bf16[512,128]{1,0:T(8,128)(2,1)}) fusion(s32[128]{0:T(128)S(1)} %get-tuple-element.26, s32[512]{0:T(512)S(1)} %add_select_fusion.1, s32[128]{0:T(128)S(1)} %get-tuple-element.27, s32[512]{0:T(512)S(1)} %add_select_fusion, pred[128]{0:T(512)(128)(4,1)S(1)} %iota_compare_fusion.1), kind=kLoop, calls=%fused_computation.6 | loop fusion | flops 458752 | bytes 398464 | tf_op jit(solution)/shard_map/convert_element_type | solution.py:198
  15.8 0.9 %select_convert_fusion.refs_3_ = bf16[512,128]{1,0:T(8,128)(2,1)} fusion(pred[512,4]{1,0:T(8,128)(4,1)S(1)} %bitcast.5, s32[512]{0:T(512)S(1)} %add_select_fusion.1), kind=kLoop, calls=%fused_computation | loop fusion | flops 262144 | bytes 135168 | tf_op jit(solution)/shard_map/convert_element_type | solution.py:194
  16.7 0.0 collective-permute-done.refs_0_
  16.7 0.0 copy-start
  16.7 0.4 collective-permute-done.1.refs_1_
  17.1 0.0 copy-start.1
  17.1 0.0 collective-permute-done.2.refs_2_
  17.1 0.0 copy-start.2
  17.1 0.3 copy-done
  17.4 0.4 copy-done.1
  17.8 0.1 copy-done.2
  17.8 13.1 %front.1 = (bf16[512,768]{1,0:T(8,128)(2,1)}, bf16[32,4,768]{2,1,0:T(4,128)(2,1)}, bf16[512,128]{1,0:T(8,128)(2,1)}) custom-call(s32[2]{0:T(128)} %pad_add_fusion.self_ref, bf16[512,768]{1,0:T(8,128)(2,1)} %patches_ref.1, bf16[136,768]{1,0:T(8,128)(2,1)} %copy-done, bf16[136,768]{1,0:T(8,128)(2,1)} %copy-done.1, bf16[136,768]{1,0:T(8,128)(2,1)} %copy-done.2, ...), custom_call_target="tpu_custom_call" | custom-call | tf_op jit(solution)/shard_map/front/pallas_call | solution.py:201
  30.9 14.6 %all_to_all.10.arrived_ref = bf16[32,4,768]{2,1,0:T(4,128)(2,1)} all-to-all(bf16[32,4,768]{2,1,0:T(4,128)(2,1)} %get-tuple-element.10), channel_id=1, replica_groups=mesh['dp'=4,'expert'=8] {'dp','expert'}, dimensions={0} | all-to-all | bytes 393216 | tf_op jit(solution)/shard_map/all_to_all | solution.py:227
  45.5 6.2 %expert.1 = bf16[32,4,768]{2,1,0:T(4,128)(2,1)} custom-call(bf16[32,4,768]{2,1,0:T(4,128)(2,1)} %all_to_all.10.arrived_ref, bf16[1,768,3072]{2,1,0:T(8,128)(2,1)} %expert_in_ref.1, bf16[1,3072,768]{2,1,0:T(8,128)(2,1)} %expert_out_ref.1), custom_call_target="tpu_custom_call" | custom-call | tf_op jit(solution)/shard_map/expert/pallas_call | solution.py:230
  51.8 11.7 %all_to_all.11.returned_ref = bf16[32,4,768]{2,1,0:T(4,128)(2,1)} all-to-all(bf16[32,4,768]{2,1,0:T(4,128)(2,1)} %expert.1), channel_id=1, replica_groups=mesh['dp'=4,'expert'=8] {'dp','expert'}, dimensions={0} | all-to-all | bytes 393216 | tf_op jit(solution)/shard_map/all_to_all | solution.py:243
  63.4 2.5 %combine.1 = bf16[512,768]{1,0:T(8,128)(2,1)} custom-call(bf16[512,768]{1,0:T(8,128)(2,1)} %get-tuple-element.8.hidden_ref, bf16[512,128]{1,0:T(8,128)(2,1)} %get-tuple-element.9.combine_ref, bf16[32,4,768]{2,1,0:T(4,128)(2,1)} %all_to_all.11.returned_ref), custom_call_target="tpu_custom_call" | custom-call | tf_op jit(solution)/shard_map/combine/pallas_call | solution.py:244
  (7 shorter events, 0.1 us)
Async XLA Ops:
  5.1 11.6 %collective-permute-start = (bf16[136,768]{1,0:T(8,128)(2,1)S(1)}, bf16[136,768]{1,0:T(8,128)(2,1)S(1)}, u32[]{:S(2)}, u32[]{:S(2)}) collective-permute-start(bf16[136,768]{1,0:T(8,128)(2,1)S(1)} %concatenate.9), channel_id=1, source_target_pairs={{0,16},{8,24},{16,0},{24,8},{1,17},{9,25},{17,1},{25,9},{2,18},{10... | collective-permute-start | bytes 626696 | tf_op jit(solution)/shard_map/ppermute | solution.py:179
  8.9 8.2 %collective-permute-start.1 = (bf16[136,768]{1,0:T(8,128)(2,1)S(1)}, bf16[136,768]{1,0:T(8,128)(2,1)S(1)}, u32[]{:S(2)}, u32[]{:S(2)}) collective-permute-start(bf16[136,768]{1,0:T(8,128)(2,1)S(1)} %concatenate.10), channel_id=1, source_target_pairs={{0,24},{8,16},{16,8},{24,0},{1,25},{9,17},{17,9},{25,1},{2,26},{10... | collective-permute-start | bytes 626696 | tf_op jit(solution)/shard_map/ppermute | solution.py:179
  9.7 7.4 %collective-permute-start.2 = (bf16[136,768]{1,0:T(8,128)(2,1)S(1)}, bf16[136,768]{1,0:T(8,128)(2,1)S(1)}, u32[]{:S(2)}, u32[]{:S(2)}) collective-permute-start(bf16[136,768]{1,0:T(8,128)(2,1)S(1)} %concatenate.11), channel_id=1, source_target_pairs={{0,8},{8,0},{16,24},{24,16},{1,9},{9,1},{17,25},{25,17},{2,10},{10... | collective-permute-start | bytes 626696 | tf_op jit(solution)/shard_map/ppermute | solution.py:179
  16.7 0.7 %copy-start = (bf16[136,768]{1,0:T(8,128)(2,1)}, bf16[136,768]{1,0:T(8,128)(2,1)S(1)}, u32[]{:S(2)}) copy-start(bf16[136,768]{1,0:T(8,128)(2,1)S(1)} %collective-permute-done.refs_0_) | copy-start | bytes 626692
  17.1 0.7 %copy-start.1 = (bf16[136,768]{1,0:T(8,128)(2,1)}, bf16[136,768]{1,0:T(8,128)(2,1)S(1)}, u32[]{:S(2)}) copy-start(bf16[136,768]{1,0:T(8,128)(2,1)S(1)} %collective-permute-done.1.refs_1_) | copy-start | bytes 626692
  17.1 0.8 %copy-start.2 = (bf16[136,768]{1,0:T(8,128)(2,1)}, bf16[136,768]{1,0:T(8,128)(2,1)S(1)}, u32[]{:S(2)}) copy-start(bf16[136,768]{1,0:T(8,128)(2,1)S(1)} %collective-permute-done.2.refs_2_) | copy-start | bytes 626692

commit v2 on v1

v2 whole, which is shorter than its diff:
```python
import functools
import math

import jax
import jax.numpy as jnp
from jax import lax
from jax.experimental import pallas as pl
from jax.experimental.pallas import tpu as pltpu
from jax.sharding import PartitionSpec as P

HEAD = 64
LANES = 128
TAG_ROWS = 8
EPS = 1e-06
NEGATIVE = -1e30
AXES = ("dp", "expert")
VMEM_LIMIT = 24 << 20


def layer_norm(values):
    centred = values - jnp.mean(values, axis=-1, keepdims=True)
    variance = jnp.mean(centred * centred, axis=-1, keepdims=True)
    return centred * lax.rsqrt(variance + EPS)


def dot(a, b, dims=((1,), (0,))):
    return lax.dot_general(a, b, (dims, ((), ())), preferred_element_type=jnp.float32)


def route_of(owner_ref, target, columns):
    blk_count = owner_ref.shape[0]
    source = jnp.int32(0)
    place = jnp.int32(-1)
    for block in range(blk_count):
        owner = owner_ref[block]
        hit = owner // (blk_count * columns) == target
        source = jnp.where(hit, block, source)
        place = jnp.where(hit, owner % blk_count, place)
    return source, place


def send_kernel(owner_ref, patches_ref, *refs, flips, columns):
    sends, sems = refs[:-1], refs[-1]
    rows = sends[0].shape[0] - TAG_ROWS
    me = lax.axis_index("dp")
    copies = []
    for n, (flip, send) in enumerate(zip(flips, sends)):
        source, place = route_of(owner_ref, me ^ flip, columns)
        at = pl.ds(pl.multiple_of(source * rows, rows), rows)
        copy = pltpu.make_async_copy(patches_ref.at[at, :], send.at[:rows, :], sems.at[n])
        copy.start()
        send[rows:, :] = jnp.full((TAG_ROWS, send.shape[1]), place.astype(jnp.float32)).astype(
            jnp.bfloat16
        )
        copies.append(copy)
    for copy in copies:
        copy.wait()


def place_block(block, place, project_in, ordered_ref, joint_ref):
    rows = block.shape[0]
    at = pl.ds(pl.multiple_of(place * rows, rows), rows)
    ordered_ref[at, :] = block
    normed = layer_norm(block.astype(jnp.float32)).astype(jnp.bfloat16)
    joint_ref[at, :] = dot(normed, project_in).astype(jnp.bfloat16)


def place_arrived(ref, project_in_ref, ordered_ref, joint_ref):
    rows = ref.shape[0] - TAG_ROWS
    place = jnp.max(ref[rows:, :LANES].astype(jnp.float32)).astype(jnp.int32)

    @pl.when(place >= 0)
    def _():
        place_block(ref[:rows, :], place, project_in_ref[...], ordered_ref, joint_ref)


def prepare_kernel(
    owner_ref,
    block_mask_ref,
    segment_ref,
    slot_keys_ref,
    patches_ref,
    near_ref,
    *refs,
    columns,
):
    count = (len(refs) - 8) // 2
    sources, weights = refs[:count], refs[count : 2 * count]
    query_mark_ref, key_mark_ref, image_ref, slot_keys_wide_ref = refs[2 * count : 2 * count + 4]
    ordered_ref, joint_ref, own_ref, sems = refs[2 * count + 4 :]
    blk_count = owner_ref.shape[0]
    tok_count = ordered_ref.shape[0]
    rows = tok_count // blk_count
    copies = [
        pltpu.make_async_copy(source, weight, sems.at[n])
        for n, (source, weight) in enumerate(zip(sources, weights))
    ]
    source, place = route_of(owner_ref, lax.axis_index("dp"), columns)
    own_at = pl.ds(pl.multiple_of(source * rows, rows), rows)
    own_copy = pltpu.make_async_copy(patches_ref.at[own_at, :], own_ref, sems.at[count])
    own_copy.start()
    for copy in copies:
        copy.start()

    lane = lax.broadcasted_iota(jnp.int32, (1, LANES), 1)
    lane_float = lane.astype(jnp.float32)
    image = (segment_ref[...] % blk_count).astype(jnp.float32)
    image = jnp.transpose(jnp.broadcast_to(image, (LANES, tok_count)))
    image_ref[...] = image
    image_is = image == lane_float
    for block in range(blk_count):
        at = slice(block * rows, (block + 1) * rows)
        blocked = jnp.zeros((1, LANES), jnp.float32)
        for other in range(blk_count):
            value = jnp.where(block_mask_ref[block, other] == 1, 0.0, NEGATIVE)
            blocked = jnp.where(lane == blk_count + other, value, blocked)
        query_mark_ref[at, :] = jnp.where(image_is[at], NEGATIVE, blocked).astype(jnp.bfloat16)
        block_is = jnp.where(lane == blk_count + block, 1.0, 0.0)
        key_mark_ref[at, :] = jnp.where(
            lane < blk_count, jnp.where(image_is[at], 0.0, 1.0), block_is
        ).astype(jnp.bfloat16)
    experts, wide = slot_keys_ref.shape[1], slot_keys_wide_ref.shape[1]
    expert = lax.broadcasted_iota(jnp.int32, (experts, wide), 0)
    column = lax.broadcasted_iota(jnp.int32, (experts, wide), 1)
    spread = jnp.where(column // blk_count == expert, 1.0, 0.0).astype(jnp.bfloat16)
    slot_keys_wide_ref[...] = dot(slot_keys_ref[...], spread).astype(jnp.bfloat16)

    own_copy.wait()
    copies[0].wait()
    project_in_ref = weights[0]
    place_block(own_ref[...], place, project_in_ref[...], ordered_ref, joint_ref)
    place_arrived(near_ref, project_in_ref, ordered_ref, joint_ref)
    for copy in copies[1:]:
        copy.wait()


def front_kernel(*refs, slots):
    arrived = refs[:slots]
    (
        _,
        _,
        query_mark_ref,
        key_mark_ref,
        image_ref,
        project_in_ref,
        project_out_ref,
        slot_keys_ref,
        ordered_ref,
        joint_ref,
        hidden_ref,
        slot_in_ref,
        combine_ref,
        context_ref,
    ) = refs[slots:]
    tok_count, width = ordered_ref.shape
    for ref in arrived:
        place_arrived(ref, project_in_ref, ordered_ref, joint_ref)

    lane = lax.broadcasted_iota(jnp.int32, (1, LANES), 1)
    first = lane < HEAD
    ones = jnp.ones((tok_count, LANES), jnp.bfloat16)
    zero = jnp.zeros((), jnp.bfloat16)
    scale = HEAD ** (-0.5) * math.log2(math.e)
    for pair in range(width // LANES):
        at = pair * LANES
        query = joint_ref[:, at : at + LANES]
        key = joint_ref[:, width + at : width + at + LANES]
        value = joint_ref[:, 2 * width + at : 2 * width + at + LANES]
        keys = jnp.concatenate([key, key_mark_ref[...]], axis=1)
        values = jnp.concatenate([value, ones], axis=1)
        parts = []
        for keep in (first, ~first):
            queries = jnp.concatenate(
                [jnp.where(keep, query, zero), query_mark_ref[...]], axis=1
            )
            scores = dot(queries, keys, ((1,), (1,)))
            top = jnp.max(scores, axis=1, keepdims=True)
            raised = jnp.exp2((scores - top) * scale).astype(jnp.bfloat16)
            parts.append(dot(raised, values))
        picked = jnp.where(first, parts[0][:, :LANES], parts[1][:, :LANES])
        total = jnp.where(first, parts[0][:, LANES:], parts[1][:, LANES:])
        context_ref[:, at : at + LANES] = (picked / total).astype(jnp.bfloat16)

    hidden = (
        ordered_ref[...].astype(jnp.float32) + dot(context_ref[...], project_out_ref[...])
    ).astype(jnp.bfloat16)
    hidden_ref[...] = hidden
    moe_normed = layer_norm(hidden.astype(jnp.float32)).astype(jnp.bfloat16)
    logits = dot(moe_normed, slot_keys_ref[...])
    blk_count = slot_in_ref.shape[1]
    image_here = image_ref[...] == (lane % blk_count).astype(jnp.float32)
    member = jnp.concatenate([image_here] * (logits.shape[1] // LANES), axis=1)
    column_top = jnp.max(jnp.where(member, logits, NEGATIVE), axis=0, keepdims=True)
    column_raised = jnp.where(member, jnp.exp(logits - column_top), 0.0)
    dispatch = column_raised / jnp.sum(column_raised, axis=0, keepdims=True)
    slot_in = dot(dispatch.astype(jnp.bfloat16), moe_normed, ((0,), (0,)))
    slot_in_ref[...] = slot_in.astype(jnp.bfloat16).reshape(slot_in_ref.shape)
    row_top = jnp.max(logits, axis=1, keepdims=True)
    row_raised = jnp.where(member, jnp.exp(logits - row_top), 0.0)
    combine = row_raised / jnp.sum(row_raised, axis=1, keepdims=True)
    combine_ref[...] = combine.astype(jnp.bfloat16)


def expert_kernel(arrived_ref, expert_in_ref, expert_out_ref, produced_ref, total_ref):
    rows, width = total_ref.shape
    slots = arrived_ref[...].reshape(rows, width)
    hidden_width = expert_in_ref.shape[2]
    step = math.gcd(hidden_width, 768)
    for at in range(0, hidden_width, step):
        inner = dot(slots, expert_in_ref[0, :, at : at + step])
        inner = 0.5 * inner * (1.0 + lax.erf(inner * math.sqrt(0.5)))
        part = dot(inner.astype(jnp.bfloat16), expert_out_ref[0, at : at + step, :])
        total_ref[...] = part if at == 0 else total_ref[...] + part
    produced_ref[...] = total_ref[...].astype(jnp.bfloat16).reshape(produced_ref.shape)


def combine_kernel(hidden_ref, combine_ref, returned_ref, out_ref):
    returned = returned_ref[...].reshape(combine_ref.shape[1], hidden_ref.shape[1])
    mixture = dot(combine_ref[...], returned)
    out_ref[...] = (hidden_ref[...].astype(jnp.float32) + mixture).astype(jnp.bfloat16)


def resident(*arrays, memory_space=pltpu.VMEM):
    return [pltpu.with_memory_space_constraint(array, memory_space) for array in arrays]


def whole(memory_space=pltpu.VMEM):
    return pl.BlockSpec(memory_space=memory_space)


def per_device(
    patches,
    owner_slot,
    segment_ids,
    block_mask,
    project_in,
    project_out,
    slot_keys,
    expert_in,
    expert_out,
):
    tok_count, width = patches.shape
    blk_count = owner_slot.shape[0]
    rows = tok_count // blk_count
    data_count = lax.axis_size("dp")
    column_count = lax.axis_size("expert")
    expert_count = slot_keys.shape[1]
    columns = expert_count * blk_count
    params = pltpu.CompilerParams(vmem_limit_bytes=VMEM_LIMIT)

    flips = [*range(2, data_count), 1]
    sends = pl.pallas_call(
        functools.partial(send_kernel, flips=flips, columns=column_count),
        out_shape=[pltpu.VMEM((rows + TAG_ROWS, width), jnp.bfloat16)] * len(flips),
        in_specs=[whole(pltpu.SMEM), whole(pltpu.HBM)],
        out_specs=[whole()] * len(flips),
        scratch_shapes=[pltpu.SemaphoreType.DMA((len(flips),))],
        compiler_params=params,
        name="send",
    )(*resident(owner_slot, patches, memory_space=pltpu.HBM))
    arrived = [
        lax.ppermute(send, "dp", [(i, i ^ flip) for i in range(data_count)])
        for flip, send in zip(flips, sends)
    ]
    far, near = arrived[:-1], arrived[-1]

    streamed = [project_in, project_out, expert_in, expert_out]
    prepared = pl.pallas_call(
        functools.partial(prepare_kernel, columns=column_count),
        out_shape=[pltpu.VMEM(w.shape, w.dtype) for w in streamed]
        + [
            pltpu.VMEM((tok_count, LANES), jnp.bfloat16),
            pltpu.VMEM((tok_count, LANES), jnp.bfloat16),
            pltpu.VMEM((tok_count, LANES), jnp.float32),
            pltpu.VMEM((width, columns), jnp.bfloat16),
            pltpu.VMEM((tok_count, width), jnp.bfloat16),
            pltpu.VMEM((tok_count, 3 * width), jnp.bfloat16),
        ],
        in_specs=[whole(pltpu.SMEM)] * 2
        + [whole()] * 2
        + [whole(pltpu.HBM), whole()]
        + [whole(pltpu.HBM)] * len(streamed),
        out_specs=[whole()] * (len(streamed) + 6),
        scratch_shapes=[
            pltpu.VMEM((rows, width), jnp.bfloat16),
            pltpu.SemaphoreType.DMA((len(streamed) + 1,)),
        ],
        compiler_params=params,
        name="prepare",
    )(
        *resident(owner_slot, block_mask, memory_space=pltpu.HBM),
        segment_ids.reshape(1, tok_count),
        slot_keys,
        *resident(patches, memory_space=pltpu.HBM),
        *resident(near),
        *resident(*streamed, memory_space=pltpu.HBM),
    )
    project_in, project_out, expert_in, expert_out = prepared[:4]
    query_mark, key_mark, image, slot_keys_wide, ordered, joint = prepared[4:]

    late = len(far)
    _, _, hidden, slot_in, combine = pl.pallas_call(
        functools.partial(front_kernel, slots=late),
        out_shape=(
            pltpu.VMEM((tok_count, width), jnp.bfloat16),
            pltpu.VMEM((tok_count, 3 * width), jnp.bfloat16),
            pltpu.VMEM((tok_count, width), jnp.bfloat16),
            pltpu.VMEM((expert_count, blk_count, width), jnp.bfloat16),
            pltpu.VMEM((tok_count, columns), jnp.bfloat16),
        ),
        in_specs=[whole()] * (8 + late),
        out_specs=(whole(),) * 5,
        input_output_aliases={late: 0, late + 1: 1},
        scratch_shapes=[pltpu.VMEM((tok_count, width), jnp.bfloat16)],
        compiler_params=params,
        name="front",
    )(
        *resident(
            *far,
            ordered,
            joint,
            query_mark,
            key_mark,
            image,
            project_in,
            project_out,
            slot_keys_wide,
        )
    )
    slots_here = lax.all_to_all(slot_in, AXES, split_axis=0, concat_axis=0, tiled=True)
    produced = pl.pallas_call(
        expert_kernel,
        out_shape=pltpu.VMEM(slots_here.shape, jnp.bfloat16),
        in_specs=[whole()] * 3,
        out_specs=whole(),
        scratch_shapes=[pltpu.VMEM((columns, width), jnp.float32)],
        compiler_params=params,
        name="expert",
    )(*resident(slots_here, expert_in, expert_out))
    returned = lax.all_to_all(produced, AXES, split_axis=0, concat_axis=0, tiled=True)
    return pl.pallas_call(
        combine_kernel,
        out_shape=jax.ShapeDtypeStruct((tok_count, width), jnp.bfloat16),
        in_specs=[whole()] * 3,
        out_specs=whole(),
        compiler_params=params,
        name="combine",
    )(*resident(hidden, combine, returned))


def solution(mesh):
    in_specs = (
        P(AXES, None),
        P(AXES),
        P(AXES),
        P(AXES, None),
        P(),
        P(),
        P(),
        P(AXES, None, None),
        P(AXES, None, None),
    )
    return jax.shard_map(
        per_device, mesh=mesh, in_specs=in_specs, out_specs=P(AXES, None), check_vma=False
    )
```

time: 66.4 us -> 51.3 us (0.77)
  other arithmetic: 5.97 us -> 0 us
  between operations: 4.49 us -> 0.06 us
  Pallas kernels: 21.8 us -> 18.8 us
  local copies, waits for them, and re-layouts: 3.71 us -> 1.64 us
  waiting for transfers between devices: 0.36 us -> 2.13 us
  blocking collectives: 26.3 us -> 25.2 us
    convert_element_type x2 -> x0, other arithmetic: 1.81 us -> none  [the longest x1 0.94 us: per_device(): member = (local_image[:, None] == column_image).astype(jnp.float32)]
    ppermute x3, waiting for transfers between devices: 0.36 us -> 2.13 us  [per_device(): lax.ppermute(send, 'dp', [(i, i ^ flip) for i in range(data_count)])]
    pallas_call x2 -> x4, Pallas kernels: 19.3 us -> 17.6 us  [the longest x1 7.71 us: per_device(): pl.pallas_call(functools.partial(front_kernel, slots=late), out_shape=(pl...]
    select_n x4 -> x0, other arithmetic: 1.37 us -> none  [the longest x1 0.69 us: per_device(): local_image = segment_ids % blk_count]
    another operation x1 -> x0, other arithmetic: 1.28 us -> none  [per_device(): self_info = jnp.stack(route(0))]
    pallas_call x1, Pallas kernels: 2.47 us -> 1.23 us  [per_device(): pl.pallas_call(combine_kernel, out_shape=jax.ShapeDtypeStruct((tok_count,...]
    dynamic_slice x1 -> x0, local copies, waits for them, and re-layouts: 1.16 us -> none  [per_device(): block = lax.dynamic_slice(patches, (source * rows, 0), (rows, width))]
    unnamed x6 -> x3, local copies, waits for them, and re-layouts: 0.76 us -> 1.64 us
  transfers between devices with their start and end apart: 3 -> 3, of which waited for: 1 -> 1; matrix products, arithmetic and copies ran while one was open for 9% -> 2% of each run, Pallas kernels for 0% -> 12%
where the time goes in v2:
time: 51.3 us; the launch traced here: 51 us
  blocking collectives  25.2 us (49%)
  Pallas kernels  18.8 us (37%)
  starting transfers between devices  3.18 us (6%)
  waiting for transfers between devices  2.13 us (4%)
  local copies, waits for them, and re-layouts  1.64 us (3%)
    all_to_all x1, blocking collectives, per_device(): lax.all_to_all(slot_in, AXES, split_axis=0, concat_axis=0, tiled=True)  13.9 us
    all_to_all x1, blocking collectives, per_device(): lax.all_to_all(produced, AXES, split_axis=0, concat_axis=0, tiled=True)  11.4 us
    pallas_call x1, Pallas kernels, per_device(): pl.pallas_call(functools.partial(front_kernel, slots=late), out_shape=(pl...  7.71 us
    pallas_call x1, Pallas kernels, per_device(): pl.pallas_call(functools.partial(prepare_kernel, columns=column_count), o...  6.13 us
    ppermute x3, starting transfers between devices, per_device(): lax.ppermute(send, 'dp', [(i, i ^ flip) for i in range(data_count)])  3.18 us
    ppermute x3, waiting for transfers between devices, per_device(): lax.ppermute(send, 'dp', [(i, i ^ flip) for i in range(data_count)])  2.13 us
    pallas_call x1, Pallas kernels, per_device(): pl.pallas_call(expert_kernel, out_shape=pltpu.VMEM(slots_here.shape, jnp....  1.88 us
    pallas_call x1, Pallas kernels, per_device(): pl.pallas_call(functools.partial(send_kernel, flips=flips, columns=column...  1.84 us
  transfers between devices with their start and end apart: 3, of which 1 were waited for; matrix products, arithmetic and copies ran while one was open for 2% of the time, Pallas kernels for 12%

profile of v2, /device:TPU:0, one launch (start us, length us, event | category | flops | bytes accessed | tf_op | source)
XLA Modules:
  0.0 51.0 jit_solution(7969192547721738085)
XLA Ops:
  0.0 1.8 %send.1 = (bf16[136,768]{1,0:T(8,128)(2,1)S(1)}, bf16[136,768]{1,0:T(8,128)(2,1)S(1)}, bf16[136,768]{1,0:T(8,128)(2,1)S(1)}) custom-call(s32[4]{0:T(128)} %owner_ref.3, bf16[512,768]{1,0:T(8,128)(2,1)} %patches_ref.3), custom_call_target="tpu_custom_call" | custom-call | tf_op jit(solution)/shard_map/send/pallas_call | solution.py:252
  1.8 0.6 %collective-permute-start.2 = (bf16[136,768]{1,0:T(8,128)(2,1)S(1)}, bf16[136,768]{1,0:T(8,128)(2,1)S(1)}, u32[]{:S(2)}, u32[]{:S(2)}) collective-permute-start(bf16[136,768]{1,0:T(8,128)(2,1)S(1)} %get-tuple-element.23), channel_id=1, source_target_pairs={{0,8},{8,0},{16,24},{24,16},{1,9},{9,1},{17,25},{25,17},{2,10},{10... | collective-permute-start | bytes 626696 | tf_op jit(solution)/shard_map/ppermute | solution.py:262
  2.4 2.6 %collective-permute-start = (bf16[136,768]{1,0:T(8,128)(2,1)S(1)}, bf16[136,768]{1,0:T(8,128)(2,1)S(1)}, u32[]{:S(2)}, u32[]{:S(2)}) collective-permute-start(bf16[136,768]{1,0:T(8,128)(2,1)S(1)} %get-tuple-element.21), channel_id=1, source_target_pairs={{0,16},{8,24},{16,0},{24,8},{1,17},{9,25},{17,1},{25,9},{2,18},{10... | collective-permute-start | bytes 626696 | tf_op jit(solution)/shard_map/ppermute | solution.py:262
  5.0 0.0 collective-permute-start.1
  5.0 1.0 %copy.12.slot_keys_ref = bf16[768,32]{1,0:T(8,128)(2,1)S(1)} copy(bf16[768,32]{0,1:T(8,128)(2,1)} %param.15) | data formatting | bytes 98304 | tf_op args[6]
  6.0 0.0 collective-permute-done.2.near_ref
  6.0 0.0 copy-start
  6.0 0.7 %copy-done = s32[512]{0:T(512)S(1)} copy-done((s32[512]{0:T(512)S(1)}, s32[512]{0:T(512)}, u32[]{:S(2)}) %copy-start) | copy-done | bytes 2072
  6.7 6.1 %prepare.1 = (bf16[768,2304]{1,0:T(8,128)(2,1)S(1)}, bf16[768,768]{1,0:T(8,128)(2,1)S(1)}, bf16[1,768,3072]{2,1,0:T(8,128)(2,1)S(1)}, bf16[1,3072,768]{2,1,0:T(8...) custom-call(s32[4]{0:T(128)} %owner_ref.3, ...), custom_call_target="tpu_custom_call" | custom-call | tf_op jit(solution)/shard_map/prepare/pallas_call | solution.py:268
  12.8 0.0 collective-permute-done.refs_0_
  12.8 2.1 %collective-permute-done.1.refs_1_ = bf16[136,768]{1,0:T(8,128)(2,1)S(1)} collective-permute-done((bf16[136,768]{1,0:T(8,128)(2,1)S(1)}, bf16[136,768]{1,0:T(8,128)(2,1)S(1)}, u32[]{:S(2)}, u32[]{:S(2)}) %collective-permute-start.1) | collective-permute-done | bytes 208928 | tf_op jit(solution)/shard_map/ppermute | solution.py:262
  15.0 7.7 %front.1 = (bf16[512,768]{1,0:T(8,128)(2,1)S(1)}, bf16[512,2304]{1,0:T(8,128)(2,1)S(1)}, bf16[512,768]{1,0:T(8,128)(2,1)S(1)}, bf16[32,4,768]{2,1,0:T(4,128)(2,1)S(1)}, bf16[512,128]{1,0:T(8,128)(2,1)S(1)}) custom-call(bf16[136,768]{1,0:T(8,128)(2,1)S(1)} %collective-permute-done.refs_0_, ...), custom_call_target="tpu_custom_call", output_to_operand_aliasing={{0}: (2, {}), {1}: (3, {})} | custom-call | tf_op jit(solution)/shard_map/front/pallas_call | solution.py:302
  22.7 13.9 %all_to_all.10.arrived_ref = bf16[32,4,768]{2,1,0:T(4,128)(2,1)S(1)} all-to-all(bf16[32,4,768]{2,1,0:T(4,128)(2,1)S(1)} %get-tuple-element.34), channel_id=1, replica_groups=mesh['dp'=4,'expert'=8] {'dp','expert'}, dimensions={0} | all-to-all | bytes 393216 | tf_op jit(solution)/shard_map/all_to_all | solution.py:330
  36.5 1.9 %expert.1 = bf16[32,4,768]{2,1,0:T(4,128)(2,1)S(1)} custom-call(bf16[32,4,768]{2,1,0:T(4,128)(2,1)S(1)} %all_to_all.10.arrived_ref, bf16[1,768,3072]{2,1,0:T(8,128)(2,1)S(1)} %get-tuple-element.35.expert_in_ref, bf16[1,3072,768]{2,1,0:T(8,128)(2,1)S(1)} %get-tuple-element.36.expert_out_ref), custom_call_target="tpu_custom_call" | custom-call | tf_op jit(solution)/shard_map/expert/pallas_call | solution.py:331
  38.4 11.4 %all_to_all.11.returned_ref = bf16[32,4,768]{2,1,0:T(4,128)(2,1)S(1)} all-to-all(bf16[32,4,768]{2,1,0:T(4,128)(2,1)S(1)} %expert.1), channel_id=1, replica_groups=mesh['dp'=4,'expert'=8] {'dp','expert'}, dimensions={0} | all-to-all | bytes 393216 | tf_op jit(solution)/shard_map/all_to_all | solution.py:340
  49.8 1.2 %combine.1 = bf16[512,768]{1,0:T(8,128)(2,1)} custom-call(bf16[512,768]{1,0:T(8,128)(2,1)S(1)} %get-tuple-element.32.hidden_ref, bf16[512,128]{1,0:T(8,128)(2,1)S(1)} %get-tuple-element.33.combine_ref, bf16[32,4,768]{2,1,0:T(4,128)(2,1)S(1)} %all_to_all.11.returned_ref), custom_call_target="tpu_custom_call" | custom-call | tf_op jit(solution)/shard_map/combine/pallas_call | solution.py:341
Async XLA Ops:
  1.8 4.1 %collective-permute-start.2 = (bf16[136,768]{1,0:T(8,128)(2,1)S(1)}, bf16[136,768]{1,0:T(8,128)(2,1)S(1)}, u32[]{:S(2)}, u32[]{:S(2)}) collective-permute-start(bf16[136,768]{1,0:T(8,128)(2,1)S(1)} %get-tuple-element.23), channel_id=1, source_target_pairs={{0,8},{8,0},{16,24},{24,16},{1,9},{9,1},{17,25},{25,17},{2,10},{10... | collective-permute-start | bytes 626696 | tf_op jit(solution)/shard_map/ppermute | solution.py:262
  2.4 10.4 %collective-permute-start = (bf16[136,768]{1,0:T(8,128)(2,1)S(1)}, bf16[136,768]{1,0:T(8,128)(2,1)S(1)}, u32[]{:S(2)}, u32[]{:S(2)}) collective-permute-start(bf16[136,768]{1,0:T(8,128)(2,1)S(1)} %get-tuple-element.21), channel_id=1, source_target_pairs={{0,16},{8,24},{16,0},{24,8},{1,17},{9,25},{17,1},{25,9},{2,18},{10... | collective-permute-start | bytes 626696 | tf_op jit(solution)/shard_map/ppermute | solution.py:262
  5.0 10.0 %collective-permute-start.1 = (bf16[136,768]{1,0:T(8,128)(2,1)S(1)}, bf16[136,768]{1,0:T(8,128)(2,1)S(1)}, u32[]{:S(2)}, u32[]{:S(2)}) collective-permute-start(bf16[136,768]{1,0:T(8,128)(2,1)S(1)} %get-tuple-element.22), channel_id=1, source_target_pairs={{0,24},{8,16},{16,8},{24,0},{1,25},{9,17},{17,9},{25,1},{2,26},{10... | collective-permute-start | bytes 626696 | tf_op jit(solution)/shard_map/ppermute | solution.py:262
  6.0 0.7 %copy-start = (s32[512]{0:T(512)S(1)}, s32[512]{0:T(512)}, u32[]{:S(2)}) copy-start(s32[512]{0:T(512)} %param.11) | copy-start | bytes 6148

commit v3 on v2

--- a/solution.py
+++ b/solution.py
@@ -57,21 +57,25 @@
         copy.wait()
 
 
-def place_block(block, place, project_in, ordered_ref, joint_ref):
+def place_block(block, place, project_in_ref, ordered_ref, joint_ref):
     rows = block.shape[0]
     at = pl.ds(pl.multiple_of(place * rows, rows), rows)
     ordered_ref[at, :] = block
     normed = layer_norm(block.astype(jnp.float32)).astype(jnp.bfloat16)
-    joint_ref[at, :] = dot(normed, project_in).astype(jnp.bfloat16)
-
-
-def place_arrived(ref, project_in_ref, ordered_ref, joint_ref):
+    joint_ref[at, :] = dot(normed, project_in_ref[...]).astype(jnp.bfloat16)
+
+
+def place_arrived(ref, project_in_ref, ordered_ref, joint_ref, certain):
     rows = ref.shape[0] - TAG_ROWS
     place = jnp.max(ref[rows:, :LANES].astype(jnp.float32)).astype(jnp.int32)
 
-    @pl.when(place >= 0)
-    def _():
-        place_block(ref[:rows, :], place, project_in_ref[...], ordered_ref, joint_ref)
+    def fill():
+        place_block(ref[:rows, :], place, project_in_ref, ordered_ref, joint_ref)
+
+    if certain:
+        fill()
+    else:
+        pl.when(place >= 0)(fill)
 
 
 def prepare_kernel(
@@ -83,6 +87,7 @@
     near_ref,
     *refs,
     columns,
+    certain,
 ):
     count = (len(refs) - 8) // 2
     sources, weights = refs[:count], refs[count : 2 * count]
@@ -119,47 +124,53 @@
         key_mark_ref[at, :] = jnp.where(
             lane < blk_count, jnp.where(image_is[at], 0.0, 1.0), block_is
         ).astype(jnp.bfloat16)
-    experts, wide = slot_keys_ref.shape[1], slot_keys_wide_ref.shape[1]
-    expert = lax.broadcasted_iota(jnp.int32, (experts, wide), 0)
-    column = lax.broadcasted_iota(jnp.int32, (experts, wide), 1)
+    wide, experts = slot_keys_wide_ref.shape[0], slot_keys_ref.shape[1]
+    column = lax.broadcasted_iota(jnp.int32, (wide, experts), 0)
+    expert = lax.broadcasted_iota(jnp.int32, (wide, experts), 1)
     spread = jnp.where(column // blk_count == expert, 1.0, 0.0).astype(jnp.bfloat16)
-    slot_keys_wide_ref[...] = dot(slot_keys_ref[...], spread).astype(jnp.bfloat16)
+    slot_keys_wide_ref[...] = dot(spread, slot_keys_ref[...], ((1,), (1,))).astype(jnp.bfloat16)
 
     own_copy.wait()
     copies[0].wait()
     project_in_ref = weights[0]
-    place_block(own_ref[...], place, project_in_ref[...], ordered_ref, joint_ref)
-    place_arrived(near_ref, project_in_ref, ordered_ref, joint_ref)
+    place_block(own_ref[...], place, project_in_ref, ordered_ref, joint_ref)
+    place_arrived(near_ref, project_in_ref, ordered_ref, joint_ref, certain)
     for copy in copies[1:]:
         copy.wait()
 
 
-def front_kernel(*refs, slots):
-    arrived = refs[:slots]
-    (
-        _,
-        _,
-        query_mark_ref,
-        key_mark_ref,
-        image_ref,
-        project_in_ref,
-        project_out_ref,
-        slot_keys_ref,
-        ordered_ref,
-        joint_ref,
-        hidden_ref,
-        slot_in_ref,
-        combine_ref,
-        context_ref,
-    ) = refs[slots:]
+def middle_kernel(*refs, certain):
+    *arrived, project_in_ref, _, _, ordered_ref, joint_ref = refs
+    for ref in arrived:
+        place_arrived(ref, project_in_ref, ordered_ref, joint_ref, certain)
+
+
+def front_kernel(
+    arrived_ref,
+    _ordered_ref,
+    _joint_ref,
+    segment_ref,
+    query_mark_ref,
+    key_mark_ref,
+    project_in_ref,
+    project_out_ref,
+    slot_keys_ref,
+    ordered_ref,
+    joint_ref,
+    hidden_ref,
+    moe_normed_ref,
+    slot_in_ref,
+    context_ref,
+    *,
+    certain,
+):
     tok_count, width = ordered_ref.shape
-    for ref in arrived:
-        place_arrived(ref, project_in_ref, ordered_ref, joint_ref)
+    place_arrived(arrived_ref, project_in_ref, ordered_ref, joint_ref, certain)
 
     lane = lax.broadcasted_iota(jnp.int32, (1, LANES), 1)
     first = lane < HEAD
+    zero = jnp.zeros((), jnp.bfloat16)
     ones = jnp.ones((tok_count, LANES), jnp.bfloat16)
-    zero = jnp.zeros((), jnp.bfloat16)
     scale = HEAD ** (-0.5) * math.log2(math.e)
     for pair in range(width // LANES):
         at = pair * LANES
@@ -181,23 +192,39 @@
         total = jnp.where(first, parts[0][:, LANES:], parts[1][:, LANES:])
         context_ref[:, at : at + LANES] = (picked / total).astype(jnp.bfloat16)
 
-    hidden = (
-        ordered_ref[...].astype(jnp.float32) + dot(context_ref[...], project_out_ref[...])
-    ).astype(jnp.bfloat16)
-    hidden_ref[...] = hidden
-    moe_normed = layer_norm(hidden.astype(jnp.float32)).astype(jnp.bfloat16)
-    logits = dot(moe_normed, slot_keys_ref[...])
+    chunk = LANES
+    made = None
+    for start in [*range(0, tok_count, chunk), None]:
+        following = None
+        if start is not None:
+            at = slice(start, start + chunk)
+            following = at, dot(context_ref[at, :], project_out_ref[...])
+        if made is not None:
+            at, projected = made
+            hidden = (ordered_ref[at, :].astype(jnp.float32) + projected).astype(jnp.bfloat16)
+            hidden_ref[at, :] = hidden
+            moe_normed_ref[at, :] = layer_norm(hidden.astype(jnp.float32)).astype(jnp.bfloat16)
+        made = following
+    moe_normed = moe_normed_ref[...]
+    logits = dot(slot_keys_ref[...], moe_normed, ((1,), (1,)))
     blk_count = slot_in_ref.shape[1]
+    column_image = lax.broadcasted_iota(jnp.int32, (logits.shape[0], 1), 0) % blk_count
+    member = segment_ref[...] % blk_count == column_image
+    top = jnp.max(jnp.where(member, logits, NEGATIVE), axis=1, keepdims=True)
+    raised = jnp.where(member, jnp.exp(logits - top), 0.0)
+    dispatch = raised / jnp.sum(raised, axis=1, keepdims=True)
+    slot_in = dot(dispatch.astype(jnp.bfloat16), moe_normed)
+    slot_in_ref[...] = slot_in.astype(jnp.bfloat16).reshape(slot_in_ref.shape)
+
+
+def weigh_kernel(moe_normed_ref, slot_keys_ref, image_ref, combine_ref, *, blk_count):
+    logits = dot(moe_normed_ref[...], slot_keys_ref[...], ((1,), (1,)))
+    lane = lax.broadcasted_iota(jnp.int32, (1, LANES), 1)
     image_here = image_ref[...] == (lane % blk_count).astype(jnp.float32)
     member = jnp.concatenate([image_here] * (logits.shape[1] // LANES), axis=1)
-    column_top = jnp.max(jnp.where(member, logits, NEGATIVE), axis=0, keepdims=True)
-    column_raised = jnp.where(member, jnp.exp(logits - column_top), 0.0)
-    dispatch = column_raised / jnp.sum(column_raised, axis=0, keepdims=True)
-    slot_in = dot(dispatch.astype(jnp.bfloat16), moe_normed, ((0,), (0,)))
-    slot_in_ref[...] = slot_in.astype(jnp.bfloat16).reshape(slot_in_ref.shape)
-    row_top = jnp.max(logits, axis=1, keepdims=True)
-    row_raised = jnp.where(member, jnp.exp(logits - row_top), 0.0)
-    combine = row_raised / jnp.sum(row_raised, axis=1, keepdims=True)
+    top = jnp.max(logits, axis=1, keepdims=True)
+    raised = jnp.where(member, jnp.exp(logits - top), 0.0)
+    combine = raised / jnp.sum(raised, axis=1, keepdims=True)
     combine_ref[...] = combine.astype(jnp.bfloat16)
 
 
@@ -246,6 +273,7 @@
     column_count = lax.axis_size("expert")
     expert_count = slot_keys.shape[1]
     columns = expert_count * blk_count
+    certain = data_count == blk_count
     params = pltpu.CompilerParams(vmem_limit_bytes=VMEM_LIMIT)
 
     flips = [*range(2, data_count), 1]
@@ -264,15 +292,16 @@
     ]
     far, near = arrived[:-1], arrived[-1]
 
+    (segment,) = resident(segment_ids.reshape(1, tok_count))
     streamed = [project_in, project_out, expert_in, expert_out]
     prepared = pl.pallas_call(
-        functools.partial(prepare_kernel, columns=column_count),
+        functools.partial(prepare_kernel, columns=column_count, certain=certain),
         out_shape=[pltpu.VMEM(w.shape, w.dtype) for w in streamed]
         + [
             pltpu.VMEM((tok_count, LANES), jnp.bfloat16),
             pltpu.VMEM((tok_count, LANES), jnp.bfloat16),
             pltpu.VMEM((tok_count, LANES), jnp.float32),
-            pltpu.VMEM((width, columns), jnp.bfloat16),
+            pltpu.VMEM((columns, width), jnp.bfloat16),
             pltpu.VMEM((tok_count, width), jnp.bfloat16),
             pltpu.VMEM((tok_count, 3 * width), jnp.bfloat16),
         ],
@@ -289,45 +318,64 @@
         name="prepare",
     )(
         *resident(owner_slot, block_mask, memory_space=pltpu.HBM),
-        segment_ids.reshape(1, tok_count),
+        segment,
         slot_keys,
         *resident(patches, memory_space=pltpu.HBM),
         *resident(near),
         *resident(*streamed, memory_space=pltpu.HBM),
     )
     project_in, project_out, expert_in, expert_out = prepared[:4]
-    query_mark, key_mark, image, slot_keys_wide, ordered, joint = prepared[4:]
-
-    late = len(far)
-    _, _, hidden, slot_in, combine = pl.pallas_call(
-        functools.partial(front_kernel, slots=late),
+    query_mark, key_mark, image, slot_keys_wide = prepared[4:8]
+    placed = prepared[8:]
+
+    placed_shapes = tuple(pltpu.VMEM(array.shape, array.dtype) for array in placed)
+    *earlier, last = far
+    if earlier:
+        base = len(earlier) + 1
+        placed = pl.pallas_call(
+            functools.partial(middle_kernel, certain=certain),
+            out_shape=placed_shapes,
+            in_specs=[whole()] * (base + 2),
+            out_specs=(whole(),) * 2,
+            input_output_aliases={base + n: n for n in range(2)},
+            compiler_params=params,
+            name="middle",
+        )(*resident(*earlier, project_in, *placed))
+    *_, hidden, moe_normed, slot_in = pl.pallas_call(
+        functools.partial(front_kernel, certain=certain),
         out_shape=(
+            *placed_shapes,
             pltpu.VMEM((tok_count, width), jnp.bfloat16),
-            pltpu.VMEM((tok_count, 3 * width), jnp.bfloat16),
             pltpu.VMEM((tok_count, width), jnp.bfloat16),
             pltpu.VMEM((expert_count, blk_count, width), jnp.bfloat16),
-            pltpu.VMEM((tok_count, columns), jnp.bfloat16),
         ),
-        in_specs=[whole()] * (8 + late),
+        in_specs=[whole()] * 9,
         out_specs=(whole(),) * 5,
-        input_output_aliases={late: 0, late + 1: 1},
+        input_output_aliases={1 + n: n for n in range(2)},
         scratch_shapes=[pltpu.VMEM((tok_count, width), jnp.bfloat16)],
         compiler_params=params,
         name="front",
     )(
         *resident(
-            *far,
-            ordered,
-            joint,
+            last,
+            *placed,
+            segment,
             query_mark,
             key_mark,
-            image,
             project_in,
             project_out,
             slot_keys_wide,
         )
     )
     slots_here = lax.all_to_all(slot_in, AXES, split_axis=0, concat_axis=0, tiled=True)
+    combine = pl.pallas_call(
+        functools.partial(weigh_kernel, blk_count=blk_count),
+        out_shape=pltpu.VMEM((tok_count, columns), jnp.bfloat16),
+        in_specs=[whole()] * 3,
+        out_specs=whole(),
+        compiler_params=params,
+        name="weigh",
+    )(*resident(moe_normed, slot_keys_wide, image))
     produced = pl.pallas_call(
         expert_kernel,
         out_shape=pltpu.VMEM(slots_here.shape, jnp.bfloat16),

time: 51.3 us -> 51 us (level)
  blocking collectives: 25.2 us -> 13.9 us
  waiting for transfers between devices: 2.13 us -> 9.05 us
  starting transfers between devices: 3.18 us -> 6.48 us
  Pallas kernels: 18.8 us -> 19.6 us
    all_to_all x1 -> x0, blocking collectives: 11.4 us -> none  [per_device(): lax.all_to_all(produced, AXES, split_axis=0, concat_axis=0, tiled=True)]
    all_to_all x0 -> x1, waiting for transfers between devices: none -> 7.73 us  [per_device(): lax.all_to_all(produced, AXES, split_axis=0, concat_axis=0, tiled=True)]
    all_to_all x0 -> x1, starting transfers between devices: none -> 3.3 us  [per_device(): lax.all_to_all(produced, AXES, split_axis=0, concat_axis=0, tiled=True)]
    ppermute x3, waiting for transfers between devices: 2.13 us -> 1.32 us  [per_device(): lax.ppermute(send, 'dp', [(i, i ^ flip) for i in range(data_count)])]
    pallas_call x1, Pallas kernels: 1.88 us -> 2.57 us  [per_device(): pl.pallas_call(expert_kernel, out_shape=pltpu.VMEM(slots_here.shape, jnp....]
    pallas_call x2 -> x4, Pallas kernels: 13.8 us -> 14 us  [the longest x1 6.52 us: per_device(): pl.pallas_call(functools.partial(front_kernel, certain=certain), out_shap...]
    unnamed x3 -> x5, local copies, waits for them, and re-layouts: 1.64 us -> 1.64 us
  transfers between devices with their start and end apart: 3 -> 4, of which waited for: 1 -> 2; matrix products, arithmetic and copies ran while one was open for 2% -> 2% of each run, Pallas kernels for 12% -> 15%
where the time goes in v3:
time: 51 us; the launch traced here: 50.7 us
  Pallas kernels  19.6 us (38%)
  blocking collectives  13.9 us (27%)
  waiting for transfers between devices  9.05 us (18%)
  starting transfers between devices  6.48 us (13%)
  local copies, waits for them, and re-layouts  1.64 us (3%)
    all_to_all x1, blocking collectives, per_device(): lax.all_to_all(slot_in, AXES, split_axis=0, concat_axis=0, tiled=True)  13.9 us
    all_to_all x1, waiting for transfers between devices, per_device(): lax.all_to_all(produced, AXES, split_axis=0, concat_axis=0, tiled=True)  7.73 us
    pallas_call x1, Pallas kernels, per_device(): pl.pallas_call(functools.partial(front_kernel, certain=certain), out_shap...  6.52 us
    pallas_call x1, Pallas kernels, per_device(): pl.pallas_call(functools.partial(prepare_kernel, columns=column_count, ce...  6.11 us
    all_to_all x1, starting transfers between devices, per_device(): lax.all_to_all(produced, AXES, split_axis=0, concat_axis=0, tiled=True)  3.3 us
    ppermute x3, starting transfers between devices, per_device(): lax.ppermute(send, 'dp', [(i, i ^ flip) for i in range(data_count)])  3.18 us
    pallas_call x1, Pallas kernels, per_device(): pl.pallas_call(expert_kernel, out_shape=pltpu.VMEM(slots_here.shape, jnp....  2.57 us
    pallas_call x1, Pallas kernels, per_device(): pl.pallas_call(functools.partial(send_kernel, flips=flips, columns=column...  1.84 us
  transfers between devices with their start and end apart: 4, of which 2 were waited for; matrix products, arithmetic and copies ran while one was open for 2% of the time, Pallas kernels for 15%

profile of v3, /device:TPU:0, one launch (start us, length us, event | category | flops | bytes accessed | tf_op | source)
XLA Modules:
  0.0 50.7 jit_solution(18127503720187552679)
XLA Ops:
  0.0 1.8 %send.1 = (bf16[136,768]{1,0:T(8,128)(2,1)S(1)}, bf16[136,768]{1,0:T(8,128)(2,1)S(1)}, bf16[136,768]{1,0:T(8,128)(2,1)S(1)}) custom-call(s32[4]{0:T(128)} %owner_ref.3, bf16[512,768]{1,0:T(8,128)(2,1)} %patches_ref.3), custom_call_target="tpu_custom_call" | custom-call | tf_op jit(solution)/shard_map/send/pallas_call | solution.py:280
  1.8 0.6 %collective-permute-start.2 = (bf16[136,768]{1,0:T(8,128)(2,1)S(1)}, bf16[136,768]{1,0:T(8,128)(2,1)S(1)}, u32[]{:S(2)}, u32[]{:S(2)}) collective-permute-start(bf16[136,768]{1,0:T(8,128)(2,1)S(1)} %get-tuple-element.25), channel_id=1, source_target_pairs={{0,8},{8,0},{16,24},{24,16},{1,9},{9,1},{17,25},{25,17},{2,10},{10... | collective-permute-start | bytes 626696 | tf_op jit(solution)/shard_map/ppermute | solution.py:290
  2.4 2.6 %collective-permute-start.1 = (bf16[136,768]{1,0:T(8,128)(2,1)S(1)}, bf16[136,768]{1,0:T(8,128)(2,1)S(1)}, u32[]{:S(2)}, u32[]{:S(2)}) collective-permute-start(bf16[136,768]{1,0:T(8,128)(2,1)S(1)} %get-tuple-element.24), channel_id=1, source_target_pairs={{0,16},{8,24},{16,0},{24,8},{1,17},{9,25},{17,1},{25,9},{2,18},{10... | collective-permute-start | bytes 626696 | tf_op jit(solution)/shard_map/ppermute | solution.py:290
  5.0 0.0 collective-permute-start
  5.0 1.0 %copy.14.slot_keys_ref = bf16[768,32]{1,0:T(8,128)(2,1)S(1)} copy(bf16[768,32]{0,1:T(8,128)(2,1)} %param.15) | data formatting | bytes 98304 | tf_op args[6]
  6.0 0.0 collective-permute-done.2.near_ref
  6.0 0.0 copy-start
  6.0 0.7 %copy-done = s32[512]{0:T(512)S(1)} copy-done((s32[512]{0:T(512)S(1)}, s32[512]{0:T(512)}, u32[]{:S(2)}) %copy-start) | copy-done | bytes 2072
  6.7 6.1 %prepare.1 = (bf16[768,2304]{1,0:T(8,128)(2,1)S(1)}, bf16[768,768]{1,0:T(8,128)(2,1)S(1)}, bf16[1,768,3072]{2,1,0:T(8,128)(2,1)S(1)}, bf16[1,3072,768]{2,1,0:T(8...) custom-call(s32[4]{0:T(128)} %owner_ref.3, ...), custom_call_target="tpu_custom_call" | custom-call | tf_op jit(solution)/shard_map/prepare/pallas_call | solution.py:297
  12.8 0.0 copy-start.1
  12.8 0.0 collective-permute-done.1.refs_0_
  12.8 0.8 %middle.1 = (bf16[512,768]{1,0:T(8,128)(2,1)S(1)}, bf16[512,2304]{1,0:T(8,128)(2,1)S(1)}) custom-call(bf16[136,768]{1,0:T(8,128)(2,1)S(1)} %collective-permute-done.1.refs_0_, bf16[768,2304]{1,0:T(8,128)(2,1)S(1)} %get-tuple-element.26.refs_1_.project_in_ref, ...), custom_call_target="tpu_custom_call", output_to_operand_aliasing={{0}: (2, {}), {1}: (3, {})} | custom-call | tf_op jit(solution)/shard_map/middle/pallas_call | solution.py:335
  13.6 1.3 %collective-permute-done.arrived_ref = bf16[136,768]{1,0:T(8,128)(2,1)S(1)} collective-permute-done((bf16[136,768]{1,0:T(8,128)(2,1)S(1)}, bf16[136,768]{1,0:T(8,128)(2,1)S(1)}, u32[]{:S(2)}, u32[]{:S(2)}) %collective-permute-start) | collective-permute-done | bytes 208928 | tf_op jit(solution)/shard_map/ppermute | solution.py:290
  15.0 0.0 copy-done.1
  15.0 6.5 %front.1 = (bf16[512,768]{1,0:T(8,128)(2,1)S(1)}, bf16[512,2304]{1,0:T(8,128)(2,1)S(1)}, bf16[512,768]{1,0:T(8,128)(2,1)S(1)}, bf16[512,768]{1,0:T(8,128)(2,1)S(1)}, bf16[32,4,768]{2,1,0:T(4,128)(2,1)S(1)}) custom-call(bf16[136,768]{1,0:T(8,128)(2,1)S(1)} %collective-permute-done.arrived_ref, ...), custom_call_target="tpu_custom_call", output_to_operand_aliasing={{0}: (1, {}), {1}: (2, {})} | custom-call | tf_op jit(solution)/shard_map/front/pallas_call | solution.py:344
  21.5 13.9 %all_to_all.10.arrived_ref = bf16[32,4,768]{2,1,0:T(4,128)(2,1)S(1)} all-to-all(bf16[32,4,768]{2,1,0:T(4,128)(2,1)S(1)} %get-tuple-element.38), channel_id=1, replica_groups=mesh['dp'=4,'expert'=8] {'dp','expert'}, dimensions={0} | all-to-all | bytes 393216 | tf_op jit(solution)/shard_map/all_to_all | solution.py:370
  35.3 2.6 %expert.1 = bf16[32,4,768]{2,1,0:T(4,128)(2,1)} custom-call(bf16[32,4,768]{2,1,0:T(4,128)(2,1)S(1)} %all_to_all.10.arrived_ref, bf16[1,768,3072]{2,1,0:T(8,128)(2,1)S(1)} %get-tuple-element.39.expert_in_ref, bf16[1,3072,768]{2,1,0:T(8,128)(2,1)S(1)} %get-tuple-element.40.expert_out_ref), custom_call_target="tpu_custom_call" | custom-call | tf_op jit(solution)/shard_map/expert/pallas_call | solution.py:379
  37.9 3.3 %all-to-all-start.1 = ((bf16[32,4,768]{2,1,0:T(4,128)(2,1)}), bf16[32,4,768]{2,1,0:T(4,128)(2,1)S(1)}, u32[]{:S(2)}, u32[]{:S(2)}) async-start(bf16[32,4,768]{2,1,0:T(4,128)(2,1)} %expert.1), calls=%async_computation.1 | async-start | bytes 393216 | tf_op jit(solution)/shard_map/all_to_all | solution.py:388
  41.2 0.5 %weigh.1.combine_ref = bf16[512,128]{1,0:T(8,128)(2,1)S(1)} custom-call(bf16[512,768]{1,0:T(8,128)(2,1)S(1)} %get-tuple-element.36.moe_normed_ref, bf16[128,768]{1,0:T(8,128)(2,1)S(1)} %get-tuple-element.34.slot_keys_ref, f32[512,128]{1,0:T(8,128)S(1)} %get-tuple-element.37.image_ref), custom_call_target="tpu_custom_call" | custom-call | tf_op jit(solution)/shard_map/weigh/pallas_call | solution.py:371
  41.8 7.7 %all-to-all-done.1.returned_ref = bf16[32,4,768]{2,1,0:T(4,128)(2,1)S(1)} async-done(((bf16[32,4,768]{2,1,0:T(4,128)(2,1)}), bf16[32,4,768]{2,1,0:T(4,128)(2,1)S(1)}, u32[]{:S(2)}, u32[]{:S(2)}) %all-to-all-start.1) | async-done | bytes 196640 | tf_op jit(solution)/shard_map/all_to_all | solution.py:388
  49.5 1.2 %combine.1 = bf16[512,768]{1,0:T(8,128)(2,1)} custom-call(bf16[512,768]{1,0:T(8,128)(2,1)S(1)} %get-tuple-element.35.hidden_ref, bf16[512,128]{1,0:T(8,128)(2,1)S(1)} %weigh.1.combine_ref, bf16[32,4,768]{2,1,0:T(4,128)(2,1)S(1)} %all-to-all-done.1.returned_ref), custom_call_target="tpu_custom_call" | custom-call | tf_op jit(solution)/shard_map/combine/pallas_call | solution.py:389
Async XLA Ops:
  1.8 4.1 %collective-permute-start.2 = (bf16[136,768]{1,0:T(8,128)(2,1)S(1)}, bf16[136,768]{1,0:T(8,128)(2,1)S(1)}, u32[]{:S(2)}, u32[]{:S(2)}) collective-permute-start(bf16[136,768]{1,0:T(8,128)(2,1)S(1)} %get-tuple-element.25), channel_id=1, source_target_pairs={{0,8},{8,0},{16,24},{24,16},{1,9},{9,1},{17,25},{25,17},{2,10},{10... | collective-permute-start | bytes 626696 | tf_op jit(solution)/shard_map/ppermute | solution.py:290
  2.4 10.4 %collective-permute-start.1 = (bf16[136,768]{1,0:T(8,128)(2,1)S(1)}, bf16[136,768]{1,0:T(8,128)(2,1)S(1)}, u32[]{:S(2)}, u32[]{:S(2)}) collective-permute-start(bf16[136,768]{1,0:T(8,128)(2,1)S(1)} %get-tuple-element.24), channel_id=1, source_target_pairs={{0,16},{8,24},{16,0},{24,8},{1,17},{9,25},{17,1},{25,9},{2,18},{10... | collective-permute-start | bytes 626696 | tf_op jit(solution)/shard_map/ppermute | solution.py:290
  5.0 10.0 %collective-permute-start = (bf16[136,768]{1,0:T(8,128)(2,1)S(1)}, bf16[136,768]{1,0:T(8,128)(2,1)S(1)}, u32[]{:S(2)}, u32[]{:S(2)}) collective-permute-start(bf16[136,768]{1,0:T(8,128)(2,1)S(1)} %get-tuple-element.23), channel_id=1, source_target_pairs={{0,24},{8,16},{16,8},{24,0},{1,25},{9,17},{17,9},{25,1},{2,26},{10... | collective-permute-start | bytes 626696 | tf_op jit(solution)/shard_map/ppermute | solution.py:290
  6.0 0.7 %copy-start = (s32[512]{0:T(512)S(1)}, s32[512]{0:T(512)}, u32[]{:S(2)}) copy-start(s32[512]{0:T(512)} %param.11) | copy-start | bytes 6148
  12.8 2.2 %copy-start.1 = (s32[512]{0:T(512)S(1)}, s32[512]{0:T(512)}, u32[]{:S(2)}) copy-start(s32[512]{0:T(512)} %param.11) | copy-start | bytes 6148
  37.9 11.6 %all-to-all-start.1 = ((bf16[32,4,768]{2,1,0:T(4,128)(2,1)}), bf16[32,4,768]{2,1,0:T(4,128)(2,1)S(1)}, u32[]{:S(2)}, u32[]{:S(2)}) async-start(bf16[32,4,768]{2,1,0:T(4,128)(2,1)} %expert.1), calls=%async_computation.1 | async-start | bytes 393216 | tf_op jit(solution)/shard_map/all_to_all | solution.py:388

commit v4 on v3

v4 whole, which is shorter than its diff:
```python
import functools
import math

import jax
import jax.numpy as jnp
from jax import lax
from jax.experimental import pallas as pl
from jax.experimental.pallas import tpu as pltpu
from jax.sharding import PartitionSpec as P


HEAD = 64
LANES = 128
SUBLANES = 8
EPS = 1e-06
NEGATIVE = -1e30
AXES = ("dp", "expert")
VMEM_LIMIT = 24 << 20


def layer_norm(values):
    centred = values - jnp.mean(values, axis=-1, keepdims=True)
    variance = jnp.mean(centred * centred, axis=-1, keepdims=True)
    return centred * lax.rsqrt(variance + EPS)


def dot(a, b, dims=((1,), (0,))):
    return lax.dot_general(a, b, (dims, ((), ())), preferred_element_type=jnp.float32)


def far_first(count):
    return [*range(2, count), 1]


def route_of(owner_ref, target, columns):
    blk_count = owner_ref.shape[0]
    source = jnp.int32(0)
    place = jnp.int32(-1)
    for block in range(blk_count):
        owner = owner_ref[block]
        hit = owner // (blk_count * columns) == target
        source = jnp.where(hit, block, source)
        place = jnp.where(hit, owner % blk_count, place)
    return source, place


def packed(block):
    rows, width = block.shape
    tiles = [
        block[:, at : at + LANES].reshape(rows // SUBLANES, SUBLANES, LANES)
        for at in range(0, width, LANES)
    ]
    return jnp.concatenate(tiles, axis=0).astype(jnp.bfloat16)


def unpacked(tiles, width):
    count = tiles.shape[0] * LANES // width
    parts = [
        tiles[at : at + count].reshape(count * SUBLANES, LANES)
        for at in range(0, tiles.shape[0], count)
    ]
    return jnp.concatenate(parts, axis=1)


def send_kernel(owner_ref, patches_ref, *refs, flips, columns):
    sends, own_ref = refs[:-1], refs[-1]
    rows = own_ref.shape[0]
    me = lax.axis_index("dp")

    def chosen(flip):
        source, place = route_of(owner_ref, me ^ flip, columns)
        return patches_ref[pl.ds(pl.multiple_of(source * rows, rows), rows), :], place

    for flip, send in zip(flips, sends):
        block, place = chosen(flip)
        tiles = send.shape[0] - 1
        send[:tiles] = packed(block.astype(jnp.float32))
        tag = jnp.full((1, SUBLANES, LANES), place.astype(jnp.float32))
        send[tiles : tiles + 1] = tag.astype(jnp.bfloat16)
    own_ref[...] = chosen(0)[0]


def place_block(block, place, project_in_ref, ordered_ref, joint_ref):
    rows = block.shape[0]
    at = pl.ds(pl.multiple_of(place * rows, rows), rows)
    ordered_ref[at, :] = block.astype(jnp.bfloat16)
    normed = layer_norm(block).astype(jnp.bfloat16)
    joint_ref[at, :] = dot(normed, project_in_ref[...]).astype(jnp.bfloat16)


def place_arrived(ref, project_in_ref, ordered_ref, joint_ref, certain):
    tiles = ref.shape[0] - 1
    place = jnp.max(ref[tiles].astype(jnp.float32)).astype(jnp.int32)

    def fill():
        block = unpacked(ref[:tiles].astype(jnp.float32), ordered_ref.shape[1])
        place_block(block, place, project_in_ref, ordered_ref, joint_ref)

    if certain:
        fill()
    else:
        pl.when(place >= 0)(fill)


def prepare_kernel(
    owner_ref,
    block_mask_ref,
    segment_ref,
    slot_keys_ref,
    own_ref,
    near_ref,
    *refs,
    columns,
    certain,
):
    count = (len(refs) - 6) // 2
    sources, weights = refs[:count], refs[count : 2 * count]
    query_mark_ref, key_mark_ref, slot_keys_wide_ref = refs[2 * count : 2 * count + 3]
    ordered_ref, joint_ref, sems = refs[2 * count + 3 :]
    blk_count = owner_ref.shape[0]
    tok_count = ordered_ref.shape[0]
    rows = own_ref.shape[0]
    copies = [
        pltpu.make_async_copy(source, weight, sems.at[n])
        for n, (source, weight) in enumerate(zip(sources, weights))
    ]
    _, place = route_of(owner_ref, lax.axis_index("dp"), columns)
    for copy in copies:
        copy.start()

    lane = lax.broadcasted_iota(jnp.int32, (1, LANES), 1)
    lane_float = lane.astype(jnp.float32)
    image = (segment_ref[...] % blk_count).astype(jnp.float32)
    image = jnp.transpose(jnp.broadcast_to(image, (LANES, tok_count)))
    image_is = image == lane_float
    for block in range(blk_count):
        at = slice(block * rows, (block + 1) * rows)
        blocked = jnp.zeros((1, LANES), jnp.float32)
        for other in range(blk_count):
            value = jnp.where(block_mask_ref[block, other] == 1, 0.0, NEGATIVE)
            blocked = jnp.where(lane == blk_count + other, value, blocked)
        query_mark_ref[at, :] = jnp.where(image_is[at], NEGATIVE, blocked).astype(jnp.bfloat16)
        block_is = jnp.where(lane == blk_count + block, 1.0, 0.0)
        key_mark_ref[at, :] = jnp.where(
            lane < blk_count, jnp.where(image_is[at], 0.0, 1.0), block_is
        ).astype(jnp.bfloat16)
    wide, experts = slot_keys_wide_ref.shape[0], slot_keys_ref.shape[1]
    column = lax.broadcasted_iota(jnp.int32, (wide, experts), 0)
    expert = lax.broadcasted_iota(jnp.int32, (wide, experts), 1)
    spread = jnp.where(column // blk_count == expert, 1.0, 0.0).astype(jnp.bfloat16)
    slot_keys_wide_ref[...] = dot(spread, slot_keys_ref[...], ((1,), (1,))).astype(jnp.bfloat16)

    copies[0].wait()
    project_in_ref = weights[0]
    place_block(own_ref[...].astype(jnp.float32), place, project_in_ref, ordered_ref, joint_ref)
    place_arrived(near_ref, project_in_ref, ordered_ref, joint_ref, certain)
    for copy in copies[1:]:
        copy.wait()


def middle_kernel(*refs, certain):
    *arrived, project_in_ref, _, _, ordered_ref, joint_ref = refs
    for ref in arrived:
        place_arrived(ref, project_in_ref, ordered_ref, joint_ref, certain)


def front_kernel(
    arrived_ref,
    _ordered_ref,
    _joint_ref,
    segment_ref,
    query_mark_ref,
    key_mark_ref,
    project_in_ref,
    project_out_ref,
    slot_keys_ref,
    expert_in_hbm,
    expert_out_hbm,
    ordered_ref,
    joint_ref,
    hidden_ref,
    slot_in_ref,
    combine_ref,
    expert_in_ref,
    expert_out_ref,
    context_ref,
    sems,
    *,
    certain,
):
    tok_count, width = ordered_ref.shape
    copies = [
        pltpu.make_async_copy(expert_in_hbm, expert_in_ref, sems.at[0]),
        pltpu.make_async_copy(expert_out_hbm, expert_out_ref, sems.at[1]),
    ]
    for copy in copies:
        copy.start()
    place_arrived(arrived_ref, project_in_ref, ordered_ref, joint_ref, certain)

    lane = lax.broadcasted_iota(jnp.int32, (1, LANES), 1)
    first = lane < HEAD
    zero = jnp.zeros((), jnp.bfloat16)
    ones = jnp.ones((tok_count, LANES), jnp.bfloat16)
    scale = HEAD ** (-0.5) * math.log2(math.e)
    for pair in range(width // LANES):
        at = pair * LANES
        query = joint_ref[:, at : at + LANES]
        key = joint_ref[:, width + at : width + at + LANES]
        value = joint_ref[:, 2 * width + at : 2 * width + at + LANES]
        keys = jnp.concatenate([key, key_mark_ref[...]], axis=1)
        values = jnp.concatenate([value, ones], axis=1)
        parts = []
        for keep in (first, ~first):
            queries = jnp.concatenate(
                [jnp.where(keep, query, zero), query_mark_ref[...]], axis=1
            )
            scores = dot(queries, keys, ((1,), (1,)))
            top = jnp.max(scores, axis=1, keepdims=True)
            raised = jnp.exp2((scores - top) * scale).astype(jnp.bfloat16)
            parts.append(dot(raised, values))
        picked = jnp.where(first, parts[0][:, :LANES], parts[1][:, :LANES])
        total = jnp.where(first, parts[0][:, LANES:], parts[1][:, LANES:])
        context_ref[:, at : at + LANES] = (picked / total).astype(jnp.bfloat16)

    hidden = (
        ordered_ref[...].astype(jnp.float32) + dot(context_ref[...], project_out_ref[...])
    ).astype(jnp.bfloat16)
    hidden_ref[...] = hidden
    moe_normed = layer_norm(hidden.astype(jnp.float32)).astype(jnp.bfloat16)
    logits = dot(slot_keys_ref[...], moe_normed, ((1,), (1,)))
    blk_count = slot_in_ref.shape[1]
    column_image = lax.broadcasted_iota(jnp.int32, (logits.shape[0], 1), 0) % blk_count
    member = segment_ref[...] % blk_count == column_image
    top = jnp.max(jnp.where(member, logits, NEGATIVE), axis=1, keepdims=True)
    raised = jnp.where(member, jnp.exp(logits - top), 0.0)
    dispatch = raised / jnp.sum(raised, axis=1, keepdims=True)
    slot_in = dot(dispatch.astype(jnp.bfloat16), moe_normed)
    slot_in_ref[...] = slot_in.astype(jnp.bfloat16).reshape(slot_in_ref.shape)
    top = jnp.max(logits, axis=0, keepdims=True)
    raised = jnp.where(member, jnp.exp(logits - top), 0.0)
    combine = raised / jnp.sum(raised, axis=0, keepdims=True)
    combine_ref[...] = jnp.transpose(combine.astype(jnp.bfloat16))
    for copy in copies:
        copy.wait()


def expert_kernel(arrived_ref, expert_in_ref, expert_out_ref, produced_ref, total_ref):
    rows, width = total_ref.shape
    slots = arrived_ref[...].reshape(rows, width)
    hidden_width = expert_in_ref.shape[2]
    step = math.gcd(hidden_width, 768)
    for at in range(0, hidden_width, step):
        inner = dot(slots, expert_in_ref[0, :, at : at + step])
        inner = 0.5 * inner * (1.0 + lax.erf(inner * math.sqrt(0.5)))
        part = dot(inner.astype(jnp.bfloat16), expert_out_ref[0, at : at + step, :])
        total_ref[...] = part if at == 0 else total_ref[...] + part
    produced_ref[...] = total_ref[...].astype(jnp.bfloat16).reshape(produced_ref.shape)


def combine_kernel(hidden_ref, combine_ref, returned_ref, out_hbm, out_ref, sems):
    returned = returned_ref[...].reshape(combine_ref.shape[1], hidden_ref.shape[1])
    count = sems.shape[0]
    rows = hidden_ref.shape[0] // count
    copies = []
    for n in range(count):
        at = slice(n * rows, (n + 1) * rows)
        mixture = dot(combine_ref[at, :], returned)
        out_ref[at, :] = (hidden_ref[at, :].astype(jnp.float32) + mixture).astype(jnp.bfloat16)
        copies.append(pltpu.make_async_copy(out_ref.at[at, :], out_hbm.at[at, :], sems.at[n]))
        copies[-1].start()
    for copy in copies:
        copy.wait()


def resident(*arrays, memory_space=pltpu.VMEM):
    return [pltpu.with_memory_space_constraint(array, memory_space) for array in arrays]


def whole(memory_space=pltpu.VMEM):
    return pl.BlockSpec(memory_space=memory_space)


def per_device(
    patches,
    owner_slot,
    segment_ids,
    block_mask,
    project_in,
    project_out,
    slot_keys,
    expert_in,
    expert_out,
):
    tok_count, width = patches.shape
    blk_count = owner_slot.shape[0]
    rows = tok_count // blk_count
    data_count = lax.axis_size("dp")
    column_count = lax.axis_size("expert")
    expert_count = slot_keys.shape[1]
    columns = expert_count * blk_count
    certain = data_count == blk_count
    params = pltpu.CompilerParams(vmem_limit_bytes=VMEM_LIMIT)

    flips = far_first(data_count)
    tiles = rows * width // (SUBLANES * LANES)
    *sends, own = pl.pallas_call(
        functools.partial(send_kernel, flips=flips, columns=column_count),
        out_shape=[pltpu.VMEM((tiles + 1, SUBLANES, LANES), jnp.bfloat16)] * len(flips)
        + [pltpu.VMEM((rows, width), jnp.bfloat16)],
        in_specs=[whole(pltpu.SMEM), whole()],
        out_specs=[whole()] * (len(flips) + 1),
        compiler_params=params,
        name="send",
    )(*resident(owner_slot, patches, memory_space=pltpu.HBM))
    arrived = []
    for flip, send in zip(flips, sends):
        arrived.append(lax.ppermute(send, "dp", [(i, i ^ flip) for i in range(data_count)]))
    far, near = arrived[:-1], arrived[-1]

    segment = segment_ids.reshape(1, tok_count)
    streamed = [project_in, project_out]
    prepared = pl.pallas_call(
        functools.partial(prepare_kernel, columns=column_count, certain=certain),
        out_shape=[pltpu.VMEM(w.shape, w.dtype) for w in streamed]
        + [
            pltpu.VMEM((tok_count, LANES), jnp.bfloat16),
            pltpu.VMEM((tok_count, LANES), jnp.bfloat16),
            pltpu.VMEM((columns, width), jnp.bfloat16),
            pltpu.VMEM((tok_count, width), jnp.bfloat16),
            pltpu.VMEM((tok_count, 3 * width), jnp.bfloat16),
        ],
        in_specs=[whole(pltpu.SMEM)] * 2
        + [whole()] * 4
        + [whole(pltpu.HBM)] * len(streamed),
        out_specs=[whole()] * (len(streamed) + 5),
        scratch_shapes=[pltpu.SemaphoreType.DMA((len(streamed),))],
        compiler_params=params,
        name="prepare",
    )(
        *resident(owner_slot, block_mask, segment, slot_keys, memory_space=pltpu.HBM),
        *resident(own, near),
        *resident(*streamed, memory_space=pltpu.HBM),
    )
    project_in, project_out = prepared[:2]
    query_mark, key_mark, slot_keys_wide = prepared[2:5]
    placed = prepared[5:]

    placed_shapes = tuple(pltpu.VMEM(array.shape, array.dtype) for array in placed)
    *earlier, last = far
    if earlier:
        base = len(earlier) + 1
        placed = pl.pallas_call(
            functools.partial(middle_kernel, certain=certain),
            out_shape=placed_shapes,
            in_specs=[whole()] * (base + 2),
            out_specs=(whole(),) * 2,
            input_output_aliases={base + n: n for n in range(2)},
            compiler_params=params,
            name="middle",
        )(*resident(*earlier, project_in, *placed))
    *_, hidden, slot_in, combine, expert_in, expert_out = pl.pallas_call(
        functools.partial(front_kernel, certain=certain),
        out_shape=(
            *placed_shapes,
            pltpu.VMEM((tok_count, width), jnp.bfloat16),
            pltpu.VMEM((expert_count, blk_count, width), jnp.bfloat16),
            pltpu.VMEM((tok_count, columns), jnp.bfloat16),
            pltpu.VMEM(expert_in.shape, jnp.bfloat16),
            pltpu.VMEM(expert_out.shape, jnp.bfloat16),
        ),
        in_specs=[whole()] * 9 + [whole(pltpu.HBM)] * 2,
        out_specs=(whole(),) * 7,
        input_output_aliases={1 + n: n for n in range(2)},
        scratch_shapes=[
            pltpu.VMEM((tok_count, width), jnp.bfloat16),
            pltpu.SemaphoreType.DMA((2,)),
        ],
        compiler_params=params,
        name="front",
    )(
        *resident(last, *placed),
        *resident(segment, memory_space=pltpu.HBM),
        *resident(query_mark, key_mark, project_in, project_out, slot_keys_wide),
        *resident(expert_in, expert_out, memory_space=pltpu.HBM),
    )
    slots_here = lax.all_to_all(slot_in, AXES, split_axis=0, concat_axis=0, tiled=True)
    produced = pl.pallas_call(
        expert_kernel,
        out_shape=pltpu.VMEM(slots_here.shape, jnp.bfloat16),
        in_specs=[whole()] * 3,
        out_specs=whole(),
        scratch_shapes=[pltpu.VMEM((columns, width), jnp.float32)],
        compiler_params=params,
        name="expert",
    )(*resident(slots_here, expert_in, expert_out))
    returned = lax.all_to_all(produced, AXES, split_axis=0, concat_axis=0, tiled=True)
    return pl.pallas_call(
        combine_kernel,
        out_shape=jax.ShapeDtypeStruct((tok_count, width), jnp.bfloat16),
        in_specs=[whole()] * 3,
        out_specs=whole(pltpu.HBM),
        scratch_shapes=[
            pltpu.VMEM((tok_count, width), jnp.bfloat16),
            pltpu.SemaphoreType.DMA((blk_count,)),
        ],
        compiler_params=params,
        name="combine",
    )(*resident(hidden, combine, returned))


def solution(mesh):
    in_specs = (
        P(AXES, None),
        P(AXES),
        P(AXES),
        P(AXES, None),
        P(),
        P(),
        P(),
        P(AXES, None, None),
        P(AXES, None, None),
    )
    return jax.shard_map(
        per_device,
        mesh=mesh,
        in_specs=in_specs,
        out_specs=P(AXES, None),
        check_vma=False,
    )
```

time: 51 us -> 50 us (0.980)
  blocking collectives: 13.9 us -> 25.2 us
  waiting for transfers between devices: 9.05 us -> 2.54 us
  starting transfers between devices: 6.48 us -> 3.18 us
  Pallas kernels: 19.6 us -> 17.1 us
    all_to_all x0 -> x1, blocking collectives: none -> 11.4 us  [per_device(): lax.all_to_all(produced, AXES, split_axis=0, concat_axis=0, tiled=True)]
    all_to_all x1 -> x0, waiting for transfers between devices: 7.73 us -> none  [per_device(): lax.all_to_all(produced, AXES, split_axis=0, concat_axis=0, tiled=True)]
    all_to_all x1 -> x0, starting transfers between devices: 3.3 us -> none  [per_device(): lax.all_to_all(produced, AXES, split_axis=0, concat_axis=0, tiled=True)]
    pallas_call x1, Pallas kernels: 6.11 us -> 4.5 us  [per_device(): pl.pallas_call(functools.partial(prepare_kernel, columns=column_count, ce...]
    ppermute x3, waiting for transfers between devices: 1.32 us -> 2.54 us  [per_device(): lax.ppermute(send, 'dp', [(i, i ^ flip) for i in range(data_count)])]
    pallas_call x1, Pallas kernels: 6.52 us -> 7.54 us  [per_device(): pl.pallas_call(functools.partial(front_kernel, certain=certain), out_shap...]
    pallas_call x1, Pallas kernels: 2.57 us -> 1.9 us  [per_device(): pl.pallas_call(expert_kernel, out_shape=pltpu.VMEM(slots_here.shape, jnp....]
    pallas_call x1, Pallas kernels: 1.84 us -> 1.26 us  [per_device(): pl.pallas_call(functools.partial(send_kernel, flips=flips, columns=column...]
  transfers between devices with their start and end apart: 4 -> 3, of which waited for: 2 -> 1; matrix products, arithmetic and copies ran while one was open for 2% -> 3% of each run, Pallas kernels for 15% -> 11%
where the time goes in v4:
time: 50 us; the launch traced here: 49.8 us
  blocking collectives  25.2 us (50%)
  Pallas kernels  17.1 us (34%)
  starting transfers between devices  3.18 us (6%)
  waiting for transfers between devices  2.54 us (5%)
  local copies, waits for them, and re-layouts  1.61 us (3%)
    all_to_all x1, blocking collectives, per_device(): lax.all_to_all(slot_in, AXES, split_axis=0, concat_axis=0, tiled=True)  13.9 us
    all_to_all x1, blocking collectives, per_device(): lax.all_to_all(produced, AXES, split_axis=0, concat_axis=0, tiled=True)  11.4 us
    pallas_call x1, Pallas kernels, per_device(): pl.pallas_call(functools.partial(front_kernel, certain=certain), out_shap...  7.54 us
    pallas_call x1, Pallas kernels, per_device(): pl.pallas_call(functools.partial(prepare_kernel, columns=column_count, ce...  4.5 us
    ppermute x3, starting transfers between devices, per_device(): lax.ppermute(send, 'dp', [(i, i ^ flip) for i in range(data_count)])  3.18 us
    ppermute x3, waiting for transfers between devices, per_device(): lax.ppermute(send, 'dp', [(i, i ^ flip) for i in range(data_count)])  2.54 us
    pallas_call x1, Pallas kernels, per_device(): pl.pallas_call(expert_kernel, out_shape=pltpu.VMEM(slots_here.shape, jnp....  1.9 us
    unnamed x1, local copies, waits for them, and re-layouts  1.61 us
  transfers between devices with their start and end apart: 3, of which 1 were waited for; matrix products, arithmetic and copies ran while one was open for 3% of the time, Pallas kernels for 11%

profile of v4, /device:TPU:0, one launch (start us, length us, event | category | flops | bytes accessed | tf_op | source)
XLA Modules:
  0.0 49.8 jit_solution(1897689050648748358)
XLA Ops:
  0.0 1.3 %send.1 = (bf16[97,8,128]{2,1,0:T(8,128)(2,1)S(1)}, bf16[97,8,128]{2,1,0:T(8,128)(2,1)S(1)}, bf16[97,8,128]{2,1,0:T(8,128)(2,1)S(1)}, bf16[128,768]{1,0:T(8,128)(2,1)S(1)}) custom-call(s32[4]{0:T(128)} %owner_ref.3, bf16[512,768]{1,0:T(8,128)(2,1)} %patches_ref.1), custom_call_target="tpu_custom_call" | custom-call | tf_op jit(solution)/shard_map/send/pallas_call | solution.py:306
  1.3 0.6 %collective-permute-start.2 = (bf16[97,8,128]{2,1,0:T(8,128)(2,1)S(1)}, bf16[97,8,128]{2,1,0:T(8,128)(2,1)S(1)}, u32[]{:S(2)}, u32[]{:S(2)}) collective-permute-start(bf16[97,8,128]{2,1,0:T(8,128)(2,1)S(1)} %get-tuple-element.26), channel_id=1, source_target_pairs={{0,8},{8,0},{16,24},{24,16},{1,9},{9,1},{17,25},{25,17},{2,10},{10... | collective-permute-start | bytes 595976 | tf_op jit(solution)/shard_map/ppermute | solution.py:317
  1.8 2.6 %collective-permute-start.1 = (bf16[97,8,128]{2,1,0:T(8,128)(2,1)S(1)}, bf16[97,8,128]{2,1,0:T(8,128)(2,1)S(1)}, u32[]{:S(2)}, u32[]{:S(2)}) collective-permute-start(bf16[97,8,128]{2,1,0:T(8,128)(2,1)S(1)} %get-tuple-element.24), channel_id=1, source_target_pairs={{0,16},{8,24},{16,0},{24,8},{1,17},{9,25},{17,1},{25,9},{2,18},{10... | collective-permute-start | bytes 595976 | tf_op jit(solution)/shard_map/ppermute | solution.py:317
  4.4 0.0 collective-permute-start
  4.5 1.6 %copy.14.slot_keys_ref = bf16[768,32]{1,0:T(8,128)(2,1)} copy(bf16[768,32]{0,1:T(8,128)(2,1)} %param.15) | data formatting | bytes 98304 | tf_op args[6]
  6.1 0.0 collective-permute-done.2.near_ref
  6.1 4.5 %prepare.1 = (bf16[768,2304]{1,0:T(8,128)(2,1)S(1)}, bf16[768,768]{1,0:T(8,128)(2,1)S(1)}, bf16[512,128]{1,0:T(8,128)(2,1)S(1)}, bf16[512,128]{1,0:T(8,128)(2,1)...) custom-call(s32[4]{0:T(128)} %owner_ref.3, ...), custom_call_target="tpu_custom_call" | custom-call | tf_op jit(solution)/shard_map/prepare/pallas_call | solution.py:322
  10.6 0.0 collective-permute-done.1.refs_0_
  10.6 0.8 %middle.1 = (bf16[512,768]{1,0:T(8,128)(2,1)S(1)}, bf16[512,2304]{1,0:T(8,128)(2,1)S(1)}) custom-call(bf16[97,8,128]{2,1,0:T(8,128)(2,1)S(1)} %collective-permute-done.1.refs_0_, bf16[768,2304]{1,0:T(8,128)(2,1)S(1)} %get-tuple-element.27.refs_1_.project_in_ref, ...), custom_call_target="tpu_custom_call", output_to_operand_aliasing={{0}: (2, {}), {1}: (3, {})} | custom-call | tf_op jit(solution)/shard_map/middle/pallas_call | solution.py:352
  11.4 2.5 %collective-permute-done.arrived_ref = bf16[97,8,128]{2,1,0:T(8,128)(2,1)S(1)} collective-permute-done((bf16[97,8,128]{2,1,0:T(8,128)(2,1)S(1)}, bf16[97,8,128]{2,1,0:T(8,128)(2,1)S(1)}, u32[]{:S(2)}, u32[]{:S(2)}) %collective-permute-start) | collective-permute-done | bytes 198688 | tf_op jit(solution)/shard_map/ppermute | solution.py:317
  13.9 7.5 %front.1 = (bf16[512,768]{1,0:T(8,128)(2,1)S(1)}, bf16[512,2304]{1,0:T(8,128)(2,1)S(1)}, bf16[512,768]{1,0:T(8,128)(2,1)S(1)}, bf16[32,4,768]{2,1,0:T(4,128)(2,1...) custom-call(bf16[97,8,128]{2,1,0:T(8,128)(2,1)S(1)} %collective-perm, ...), custom_call_target="tpu_custom_call", output_to_operand_aliasing={{0}: (1, {}), {1}: (2, {})} | custom-call | tf_op jit(solution)/shard_map/front/pallas_call | solution.py:361
  21.5 13.9 %all_to_all.10.arrived_ref = bf16[32,4,768]{2,1,0:T(4,128)(2,1)S(1)} all-to-all(bf16[32,4,768]{2,1,0:T(4,128)(2,1)S(1)} %get-tuple-element.38), channel_id=1, replica_groups=mesh['dp'=4,'expert'=8] {'dp','expert'}, dimensions={0} | all-to-all | bytes 393216 | tf_op jit(solution)/shard_map/all_to_all | solution.py:386
  35.4 1.9 %expert.1 = bf16[32,4,768]{2,1,0:T(4,128)(2,1)S(1)} custom-call(bf16[32,4,768]{2,1,0:T(4,128)(2,1)S(1)} %all_to_all.10.arrived_ref, bf16[1,768,3072]{2,1,0:T(8,128)(2,1)S(1)} %get-tuple-element.39.expert_in_ref, bf16[1,3072,768]{2,1,0:T(8,128)(2,1)S(1)} %get-tuple-element.40.expert_out_ref), custom_call_target="tpu_custom_call" | custom-call | tf_op jit(solution)/shard_map/expert/pallas_call | solution.py:387
  37.3 11.4 %all_to_all.11.returned_ref = bf16[32,4,768]{2,1,0:T(4,128)(2,1)S(1)} all-to-all(bf16[32,4,768]{2,1,0:T(4,128)(2,1)S(1)} %expert.1), channel_id=1, replica_groups=mesh['dp'=4,'expert'=8] {'dp','expert'}, dimensions={0} | all-to-all | bytes 393216 | tf_op jit(solution)/shard_map/all_to_all | solution.py:396
  48.6 1.1 %combine.1 = bf16[512,768]{1,0:T(8,128)(2,1)} custom-call(bf16[512,768]{1,0:T(8,128)(2,1)S(1)} %get-tuple-element.36.hidden_ref, bf16[512,128]{1,0:T(8,128)(2,1)S(1)} %get-tuple-element.37.combine_ref, bf16[32,4,768]{2,1,0:T(4,128)(2,1)S(1)} %all_to_all.11.returned_ref), custom_call_target="tpu_custom_call" | custom-call | tf_op jit(solution)/shard_map/combine/pallas_call | solution.py:397
Async XLA Ops:
  1.3 4.8 %collective-permute-start.2 = (bf16[97,8,128]{2,1,0:T(8,128)(2,1)S(1)}, bf16[97,8,128]{2,1,0:T(8,128)(2,1)S(1)}, u32[]{:S(2)}, u32[]{:S(2)}) collective-permute-start(bf16[97,8,128]{2,1,0:T(8,128)(2,1)S(1)} %get-tuple-element.26), channel_id=1, source_target_pairs={{0,8},{8,0},{16,24},{24,16},{1,9},{9,1},{17,25},{25,17},{2,10},{10... | collective-permute-start | bytes 595976 | tf_op jit(solution)/shard_map/ppermute | solution.py:317
  1.8 8.8 %collective-permute-start.1 = (bf16[97,8,128]{2,1,0:T(8,128)(2,1)S(1)}, bf16[97,8,128]{2,1,0:T(8,128)(2,1)S(1)}, u32[]{:S(2)}, u32[]{:S(2)}) collective-permute-start(bf16[97,8,128]{2,1,0:T(8,128)(2,1)S(1)} %get-tuple-element.24), channel_id=1, source_target_pairs={{0,16},{8,24},{16,0},{24,8},{1,17},{9,25},{17,1},{25,9},{2,18},{10... | collective-permute-start | bytes 595976 | tf_op jit(solution)/shard_map/ppermute | solution.py:317
  4.4 9.5 %collective-permute-start = (bf16[97,8,128]{2,1,0:T(8,128)(2,1)S(1)}, bf16[97,8,128]{2,1,0:T(8,128)(2,1)S(1)}, u32[]{:S(2)}, u32[]{:S(2)}) collective-permute-start(bf16[97,8,128]{2,1,0:T(8,128)(2,1)S(1)} %get-tuple-element.23), channel_id=1, source_target_pairs={{0,24},{8,16},{16,8},{24,0},{1,25},{9,17},{17,9},{25,1},{2,26},{10... | collective-permute-start | bytes 595976 | tf_op jit(solution)/shard_map/ppermute | solution.py:317

commit v5 on v4

--- a/solution.py
+++ b/solution.py
@@ -109,28 +109,37 @@
     slot_keys_ref,
     own_ref,
     near_ref,
-    *refs,
+    project_in_hbm,
+    project_out_hbm,
+    project_in_ref,
+    project_out_ref,
+    image_ref,
+    query_mark_ref,
+    key_mark_ref,
+    slot_keys_wide_ref,
+    ordered_ref,
+    joint_ref,
+    sems,
+    *,
     columns,
     certain,
 ):
-    count = (len(refs) - 6) // 2
-    sources, weights = refs[:count], refs[count : 2 * count]
-    query_mark_ref, key_mark_ref, slot_keys_wide_ref = refs[2 * count : 2 * count + 3]
-    ordered_ref, joint_ref, sems = refs[2 * count + 3 :]
     blk_count = owner_ref.shape[0]
     tok_count = ordered_ref.shape[0]
     rows = own_ref.shape[0]
     copies = [
-        pltpu.make_async_copy(source, weight, sems.at[n])
-        for n, (source, weight) in enumerate(zip(sources, weights))
+        pltpu.make_async_copy(project_in_hbm, project_in_ref, sems.at[0]),
+        pltpu.make_async_copy(project_out_hbm, project_out_ref, sems.at[1]),
     ]
-    _, place = route_of(owner_ref, lax.axis_index("dp"), columns)
     for copy in copies:
         copy.start()
+    _, place = route_of(owner_ref, lax.axis_index("dp"), columns)
 
     lane = lax.broadcasted_iota(jnp.int32, (1, LANES), 1)
     lane_float = lane.astype(jnp.float32)
-    image = (segment_ref[...] % blk_count).astype(jnp.float32)
+    image = segment_ref[...] % blk_count
+    image_ref[...] = image
+    image = image.astype(jnp.float32)
     image = jnp.transpose(jnp.broadcast_to(image, (LANES, tok_count)))
     image_is = image == lane_float
     for block in range(blk_count):
@@ -151,11 +160,9 @@
     slot_keys_wide_ref[...] = dot(spread, slot_keys_ref[...], ((1,), (1,))).astype(jnp.bfloat16)
 
     copies[0].wait()
-    project_in_ref = weights[0]
     place_block(own_ref[...].astype(jnp.float32), place, project_in_ref, ordered_ref, joint_ref)
     place_arrived(near_ref, project_in_ref, ordered_ref, joint_ref, certain)
-    for copy in copies[1:]:
-        copy.wait()
+    copies[1].wait()
 
 
 def middle_kernel(*refs, certain):
@@ -168,7 +175,7 @@
     arrived_ref,
     _ordered_ref,
     _joint_ref,
-    segment_ref,
+    image_ref,
     query_mark_ref,
     key_mark_ref,
     project_in_ref,
@@ -230,7 +237,7 @@
     logits = dot(slot_keys_ref[...], moe_normed, ((1,), (1,)))
     blk_count = slot_in_ref.shape[1]
     column_image = lax.broadcasted_iota(jnp.int32, (logits.shape[0], 1), 0) % blk_count
-    member = segment_ref[...] % blk_count == column_image
+    member = image_ref[...] == column_image
     top = jnp.max(jnp.where(member, logits, NEGATIVE), axis=1, keepdims=True)
     raised = jnp.where(member, jnp.exp(logits - top), 0.0)
     dispatch = raised / jnp.sum(raised, axis=1, keepdims=True)
@@ -318,32 +325,29 @@
     far, near = arrived[:-1], arrived[-1]
 
     segment = segment_ids.reshape(1, tok_count)
-    streamed = [project_in, project_out]
     prepared = pl.pallas_call(
         functools.partial(prepare_kernel, columns=column_count, certain=certain),
-        out_shape=[pltpu.VMEM(w.shape, w.dtype) for w in streamed]
-        + [
+        out_shape=[
+            pltpu.VMEM(project_in.shape, jnp.bfloat16),
+            pltpu.VMEM(project_out.shape, jnp.bfloat16),
+            pltpu.VMEM((1, tok_count), jnp.int32),
             pltpu.VMEM((tok_count, LANES), jnp.bfloat16),
             pltpu.VMEM((tok_count, LANES), jnp.bfloat16),
             pltpu.VMEM((columns, width), jnp.bfloat16),
             pltpu.VMEM((tok_count, width), jnp.bfloat16),
             pltpu.VMEM((tok_count, 3 * width), jnp.bfloat16),
         ],
-        in_specs=[whole(pltpu.SMEM)] * 2
-        + [whole()] * 4
-        + [whole(pltpu.HBM)] * len(streamed),
-        out_specs=[whole()] * (len(streamed) + 5),
-        scratch_shapes=[pltpu.SemaphoreType.DMA((len(streamed),))],
+        in_specs=[whole(pltpu.SMEM)] * 2 + [whole()] * 4 + [whole(pltpu.HBM)] * 2,
+        out_specs=[whole()] * 8,
+        scratch_shapes=[pltpu.SemaphoreType.DMA((2,))],
         compiler_params=params,
         name="prepare",
     )(
         *resident(owner_slot, block_mask, segment, slot_keys, memory_space=pltpu.HBM),
         *resident(own, near),
-        *resident(*streamed, memory_space=pltpu.HBM),
+        *resident(project_in, project_out, memory_space=pltpu.HBM),
     )
-    project_in, project_out = prepared[:2]
-    query_mark, key_mark, slot_keys_wide = prepared[2:5]
-    placed = prepared[5:]
+    project_in, project_out, image, query_mark, key_mark, slot_keys_wide, *placed = prepared
 
     placed_shapes = tuple(pltpu.VMEM(array.shape, array.dtype) for array in placed)
     *earlier, last = far
@@ -378,9 +382,8 @@
         compiler_params=params,
         name="front",
     )(
-        *resident(last, *placed),
-        *resident(segment, memory_space=pltpu.HBM),
-        *resident(query_mark, key_mark, project_in, project_out, slot_keys_wide),
+        *resident(last, *placed, image, query_mark, key_mark),
+        *resident(project_in, project_out, slot_keys_wide),
         *resident(expert_in, expert_out, memory_space=pltpu.HBM),
     )
     slots_here = lax.all_to_all(slot_in, AXES, split_axis=0, concat_axis=0, tiled=True)

time: 50 us -> 49.3 us (0.986)
  Pallas kernels: 17.1 us -> 16.4 us
    pallas_call x1, Pallas kernels: 7.54 us -> 6.85 us  [per_device(): pl.pallas_call(functools.partial(front_kernel, certain=certain), out_shap...]
where the time goes in v5:
time: 49.3 us; the launch traced here: 49.1 us
  blocking collectives  25.2 us (51%)
  Pallas kernels  16.4 us (33%)
  starting transfers between devices  3.18 us (6%)
  waiting for transfers between devices  2.62 us (5%)
  local copies, waits for them, and re-layouts  1.61 us (3%)
    all_to_all x1, blocking collectives, per_device(): lax.all_to_all(slot_in, AXES, split_axis=0, concat_axis=0, tiled=True)  13.9 us
    all_to_all x1, blocking collectives, per_device(): lax.all_to_all(produced, AXES, split_axis=0, concat_axis=0, tiled=True)  11.4 us
    pallas_call x1, Pallas kernels, per_device(): pl.pallas_call(functools.partial(front_kernel, certain=certain), out_shap...  6.85 us
    pallas_call x1, Pallas kernels, per_device(): pl.pallas_call(functools.partial(prepare_kernel, columns=column_count, ce...  4.41 us
    ppermute x3, starting transfers between devices, per_device(): lax.ppermute(send, 'dp', [(i, i ^ flip) for i in range(data_count)])  3.18 us
    ppermute x3, waiting for transfers between devices, per_device(): lax.ppermute(send, 'dp', [(i, i ^ flip) for i in range(data_count)])  2.62 us
    pallas_call x1, Pallas kernels, per_device(): pl.pallas_call(expert_kernel, out_shape=pltpu.VMEM(slots_here.shape, jnp....  1.93 us
    unnamed x1, local copies, waits for them, and re-layouts  1.61 us
  transfers between devices with their start and end apart: 3, of which 1 were waited for; matrix products, arithmetic and copies ran while one was open for 3% of the time, Pallas kernels for 11%

profile of v5, /device:TPU:0, one launch (start us, length us, event | category | flops | bytes accessed | tf_op | source)
XLA Modules:
  0.0 49.1 jit_solution(2017392991094220540)
XLA Ops:
  0.0 1.3 %send.1 = (bf16[97,8,128]{2,1,0:T(8,128)(2,1)S(1)}, bf16[97,8,128]{2,1,0:T(8,128)(2,1)S(1)}, bf16[97,8,128]{2,1,0:T(8,128)(2,1)S(1)}, bf16[128,768]{1,0:T(8,128)(2,1)S(1)}) custom-call(s32[4]{0:T(128)} %owner_ref.3, bf16[512,768]{1,0:T(8,128)(2,1)} %patches_ref.1), custom_call_target="tpu_custom_call" | custom-call | tf_op jit(solution)/shard_map/send/pallas_call | solution.py:313
  1.3 0.6 %collective-permute-start.2 = (bf16[97,8,128]{2,1,0:T(8,128)(2,1)S(1)}, bf16[97,8,128]{2,1,0:T(8,128)(2,1)S(1)}, u32[]{:S(2)}, u32[]{:S(2)}) collective-permute-start(bf16[97,8,128]{2,1,0:T(8,128)(2,1)S(1)} %get-tuple-element.27), channel_id=1, source_target_pairs={{0,8},{8,0},{16,24},{24,16},{1,9},{9,1},{17,25},{25,17},{2,10},{10... | collective-permute-start | bytes 595976 | tf_op jit(solution)/shard_map/ppermute | solution.py:324
  1.8 2.6 %collective-permute-start.1 = (bf16[97,8,128]{2,1,0:T(8,128)(2,1)S(1)}, bf16[97,8,128]{2,1,0:T(8,128)(2,1)S(1)}, u32[]{:S(2)}, u32[]{:S(2)}) collective-permute-start(bf16[97,8,128]{2,1,0:T(8,128)(2,1)S(1)} %get-tuple-element.25), channel_id=1, source_target_pairs={{0,16},{8,24},{16,0},{24,8},{1,17},{9,25},{17,1},{25,9},{2,18},{10... | collective-permute-start | bytes 595976 | tf_op jit(solution)/shard_map/ppermute | solution.py:324
  4.4 0.0 collective-permute-start
  4.5 1.6 %copy.14.slot_keys_ref = bf16[768,32]{1,0:T(8,128)(2,1)} copy(bf16[768,32]{0,1:T(8,128)(2,1)} %param.15) | data formatting | bytes 98304 | tf_op args[6]
  6.1 0.0 collective-permute-done.2.near_ref
  6.1 4.4 %prepare.1 = (bf16[768,2304]{1,0:T(8,128)(2,1)S(1)}, bf16[768,768]{1,0:T(8,128)(2,1)S(1)}, s32[1,512]{1,0:T(1,128)S(1)}, bf16[512,128]{1,0:T(8,128)(2,1)S(1)}, b...) custom-call(s32[4]{0:T(128)} %owner_ref.3, ...), custom_call_target="tpu_custom_call" | custom-call | tf_op jit(solution)/shard_map/prepare/pallas_call | solution.py:328
  10.5 0.0 collective-permute-done.1.refs_0_
  10.5 0.8 %middle.1 = (bf16[512,768]{1,0:T(8,128)(2,1)S(1)}, bf16[512,2304]{1,0:T(8,128)(2,1)S(1)}) custom-call(bf16[97,8,128]{2,1,0:T(8,128)(2,1)S(1)} %collective-permute-done.1.refs_0_, bf16[768,2304]{1,0:T(8,128)(2,1)S(1)} %get-tuple-element.28.refs_1_.project_in_ref, ...), custom_call_target="tpu_custom_call", output_to_operand_aliasing={{0}: (2, {}), {1}: (3, {})} | custom-call | tf_op jit(solution)/shard_map/middle/pallas_call | solution.py:356
  11.3 2.6 %collective-permute-done.arrived_ref = bf16[97,8,128]{2,1,0:T(8,128)(2,1)S(1)} collective-permute-done((bf16[97,8,128]{2,1,0:T(8,128)(2,1)S(1)}, bf16[97,8,128]{2,1,0:T(8,128)(2,1)S(1)}, u32[]{:S(2)}, u32[]{:S(2)}) %collective-permute-start) | collective-permute-done | bytes 198688 | tf_op jit(solution)/shard_map/ppermute | solution.py:324
  13.9 6.9 %front.1 = (bf16[512,768]{1,0:T(8,128)(2,1)S(1)}, bf16[512,2304]{1,0:T(8,128)(2,1)S(1)}, bf16[512,768]{1,0:T(8,128)(2,1)S(1)}, bf16[32,4,768]{2,1,0:T(4,128)(2,1...) custom-call(bf16[97,8,128]{2,1,0:T(8,128)(2,1)S(1)} %collective-perm, ...), custom_call_target="tpu_custom_call", output_to_operand_aliasing={{0}: (1, {}), {1}: (2, {})} | custom-call | tf_op jit(solution)/shard_map/front/pallas_call | solution.py:365
  20.8 13.9 %all_to_all.10.arrived_ref = bf16[32,4,768]{2,1,0:T(4,128)(2,1)S(1)} all-to-all(bf16[32,4,768]{2,1,0:T(4,128)(2,1)S(1)} %get-tuple-element.40), channel_id=1, replica_groups=mesh['dp'=4,'expert'=8] {'dp','expert'}, dimensions={0} | all-to-all | bytes 393216 | tf_op jit(solution)/shard_map/all_to_all | solution.py:389
  34.7 1.9 %expert.1 = bf16[32,4,768]{2,1,0:T(4,128)(2,1)S(1)} custom-call(bf16[32,4,768]{2,1,0:T(4,128)(2,1)S(1)} %all_to_all.10.arrived_ref, bf16[1,768,3072]{2,1,0:T(8,128)(2,1)S(1)} %get-tuple-element.41.expert_in_ref, bf16[1,3072,768]{2,1,0:T(8,128)(2,1)S(1)} %get-tuple-element.42.expert_out_ref), custom_call_target="tpu_custom_call" | custom-call | tf_op jit(solution)/shard_map/expert/pallas_call | solution.py:390
  36.6 11.4 %all_to_all.11.returned_ref = bf16[32,4,768]{2,1,0:T(4,128)(2,1)S(1)} all-to-all(bf16[32,4,768]{2,1,0:T(4,128)(2,1)S(1)} %expert.1), channel_id=1, replica_groups=mesh['dp'=4,'expert'=8] {'dp','expert'}, dimensions={0} | all-to-all | bytes 393216 | tf_op jit(solution)/shard_map/all_to_all | solution.py:399
  48.0 1.1 %combine.1 = bf16[512,768]{1,0:T(8,128)(2,1)} custom-call(bf16[512,768]{1,0:T(8,128)(2,1)S(1)} %get-tuple-element.38.hidden_ref, bf16[512,128]{1,0:T(8,128)(2,1)S(1)} %get-tuple-element.39.combine_ref, bf16[32,4,768]{2,1,0:T(4,128)(2,1)S(1)} %all_to_all.11.returned_ref), custom_call_target="tpu_custom_call" | custom-call | tf_op jit(solution)/shard_map/combine/pallas_call | solution.py:400
Async XLA Ops:
  1.3 4.8 %collective-permute-start.2 = (bf16[97,8,128]{2,1,0:T(8,128)(2,1)S(1)}, bf16[97,8,128]{2,1,0:T(8,128)(2,1)S(1)}, u32[]{:S(2)}, u32[]{:S(2)}) collective-permute-start(bf16[97,8,128]{2,1,0:T(8,128)(2,1)S(1)} %get-tuple-element.27), channel_id=1, source_target_pairs={{0,8},{8,0},{16,24},{24,16},{1,9},{9,1},{17,25},{25,17},{2,10},{10... | collective-permute-start | bytes 595976 | tf_op jit(solution)/shard_map/ppermute | solution.py:324
  1.8 8.7 %collective-permute-start.1 = (bf16[97,8,128]{2,1,0:T(8,128)(2,1)S(1)}, bf16[97,8,128]{2,1,0:T(8,128)(2,1)S(1)}, u32[]{:S(2)}, u32[]{:S(2)}) collective-permute-start(bf16[97,8,128]{2,1,0:T(8,128)(2,1)S(1)} %get-tuple-element.25), channel_id=1, source_target_pairs={{0,16},{8,24},{16,0},{24,8},{1,17},{9,25},{17,1},{25,9},{2,18},{10... | collective-permute-start | bytes 595976 | tf_op jit(solution)/shard_map/ppermute | solution.py:324
  4.4 9.5 %collective-permute-start = (bf16[97,8,128]{2,1,0:T(8,128)(2,1)S(1)}, bf16[97,8,128]{2,1,0:T(8,128)(2,1)S(1)}, u32[]{:S(2)}, u32[]{:S(2)}) collective-permute-start(bf16[97,8,128]{2,1,0:T(8,128)(2,1)S(1)} %get-tuple-element.24), channel_id=1, source_target_pairs={{0,24},{8,16},{16,8},{24,0},{1,25},{9,17},{17,9},{25,1},{2,26},{10... | collective-permute-start | bytes 595976 | tf_op jit(solution)/shard_map/ppermute | solution.py:324

commit v6 on v5

--- a/solution.py
+++ b/solution.py
@@ -80,26 +80,135 @@
     own_ref[...] = chosen(0)[0]
 
 
-def place_block(block, place, project_in_ref, ordered_ref, joint_ref):
-    rows = block.shape[0]
-    at = pl.ds(pl.multiple_of(place * rows, rows), rows)
+def block_at(index, rows):
+    if isinstance(index, int):
+        return slice(index * rows, (index + 1) * rows)
+    return pl.ds(pl.multiple_of(index * rows, rows), rows)
+
+
+def place_block(block, index, project_in_ref, ordered_ref, joint_ref):
+    at = block_at(index, block.shape[0])
     ordered_ref[at, :] = block.astype(jnp.bfloat16)
     normed = layer_norm(block).astype(jnp.bfloat16)
     joint_ref[at, :] = dot(normed, project_in_ref[...]).astype(jnp.bfloat16)
 
 
-def place_arrived(ref, project_in_ref, ordered_ref, joint_ref, certain):
+def place_arrived(ref, slot, project_in_ref, ordered_ref, joint_ref):
     tiles = ref.shape[0] - 1
     place = jnp.max(ref[tiles].astype(jnp.float32)).astype(jnp.int32)
 
-    def fill():
+    def fill(index):
         block = unpacked(ref[:tiles].astype(jnp.float32), ordered_ref.shape[1])
-        place_block(block, place, project_in_ref, ordered_ref, joint_ref)
-
-    if certain:
-        fill()
+        place_block(block, index, project_in_ref, ordered_ref, joint_ref)
+
+    if slot is not None:
+        fill(slot)
     else:
-        pl.when(place >= 0)(fill)
+        pl.when(place >= 0)(lambda: fill(place))
+    return place
+
+
+def read_place(places_ref, slot):
+    return jnp.max(places_ref[slot : slot + 1, :]).astype(jnp.int32)
+
+
+def note_place(places_ref, slot, place):
+    places_ref[slot : slot + 1, :] = jnp.full((1, LANES), place.astype(jnp.float32))
+
+
+def gathered(mark_ref, places, rows):
+    return jnp.concatenate([mark_ref[block_at(place, rows), :] for place in places], axis=0)
+
+
+class Attention:
+    def __init__(self, joint_ref, query_mark, key_mark):
+        self.joint_ref, self.query_mark, self.key_mark = joint_ref, query_mark, key_mark
+        self.width = joint_ref.shape[1] // 3
+        self.scale = HEAD ** (-0.5) * math.log2(math.e)
+        first = lax.broadcasted_iota(jnp.int32, (1, LANES), 1) < HEAD
+        self.first, self.keeps = first, (first, ~first)
+        self.zero = jnp.zeros((), jnp.bfloat16)
+
+    def part(self, which, pair, rows):
+        at = which * self.width + pair * LANES
+        return self.joint_ref[rows, at : at + LANES]
+
+    def begin(self, finish, pair, start, stop, keys_stop):
+        query = self.part(0, pair, slice(start, stop))
+        span = slice(0, keys_stop)
+        keys = jnp.concatenate([self.part(1, pair, span), self.key_mark[span]], axis=1)
+        ones = jnp.ones((keys_stop, LANES), jnp.bfloat16)
+        values = jnp.concatenate([self.part(2, pair, span), ones], axis=1)
+        scores = []
+        for keep in self.keeps:
+            queries = jnp.concatenate(
+                [jnp.where(keep, query, self.zero), self.query_mark[start:stop]], axis=1
+            )
+            scores.append(dot(queries, keys, ((1,), (1,))))
+        yield
+        tops = [jnp.max(part, axis=1, keepdims=True) for part in scores]
+        raised = [
+            jnp.exp2((part - top) * self.scale).astype(jnp.bfloat16)
+            for part, top in zip(scores, tops)
+        ]
+        yield
+        parts = [dot(part, values) for part in raised]
+        picked = jnp.where(self.first, parts[0][:, :LANES], parts[1][:, :LANES])
+        total = jnp.where(self.first, parts[0][:, LANES:], parts[1][:, LANES:])
+        finish(tops, picked, total)
+
+    def extend(self, finish, pair, stop, block, old):
+        queries = jnp.concatenate(
+            [self.part(0, pair, slice(0, stop)), self.query_mark[:stop]], axis=1
+        )
+        key, value = self.part(1, pair, block), self.part(2, pair, block)
+        one = jnp.ones_like(value)
+        keys = [
+            jnp.concatenate([jnp.where(keep, key, self.zero), self.key_mark[block]], axis=1)
+            for keep in self.keeps
+        ]
+        values = [
+            jnp.concatenate(
+                [jnp.where(keep, value, self.zero), jnp.where(keep, one, self.zero)], axis=1
+            )
+            for keep in self.keeps
+        ]
+        scores = dot(queries, jnp.concatenate(keys, axis=0), ((1,), (1,)))
+        yield
+        olds, picked, total = old()
+        count = key.shape[0]
+        tops, raised, fades = [], [], []
+        for head, old in enumerate(olds):
+            here = scores[:, head * count : (head + 1) * count]
+            top = jnp.maximum(old, jnp.max(here, axis=1, keepdims=True))
+            raised.append(jnp.exp2((here - top) * self.scale).astype(jnp.bfloat16))
+            fades.append(jnp.exp2((old - top) * self.scale))
+            tops.append(top)
+        yield
+        added = dot(jnp.concatenate(raised, axis=1), jnp.concatenate(values, axis=0))
+        fade = jnp.where(self.first, fades[0], fades[1])
+        finish(tops, picked * fade + added[:, :LANES], total * fade + added[:, LANES:])
+
+
+def staggered(tasks):
+    running = []
+    for task in [*tasks, None, None]:
+        running = ([task] if task else []) + running
+        running = [one for one in running if next(one, running) is None]
+
+
+def keep_state(state, pair, rows, tops, picked, total):
+    top_ref, picked_ref, total_ref = state
+    for head, top in enumerate(tops):
+        top_ref[2 * pair + head, rows, :] = jnp.broadcast_to(top, picked.shape)
+    picked_ref[pair, rows, :] = picked
+    total_ref[pair, rows, :] = total
+
+
+def read_state(state, pair, rows):
+    top_ref, picked_ref, total_ref = state
+    tops = [top_ref[2 * pair + head, rows, :] for head in range(2)]
+    return tops, picked_ref[pair, rows, :], total_ref[pair, rows, :]
 
 
 def prepare_kernel(
@@ -119,6 +228,10 @@
     slot_keys_wide_ref,
     ordered_ref,
     joint_ref,
+    places_ref,
+    top_ref,
+    picked_ref,
+    total_ref,
     sems,
     *,
     columns,
@@ -133,7 +246,7 @@
     ]
     for copy in copies:
         copy.start()
-    _, place = route_of(owner_ref, lax.axis_index("dp"), columns)
+    _, own_place = route_of(owner_ref, lax.axis_index("dp"), columns)
 
     lane = lax.broadcasted_iota(jnp.int32, (1, LANES), 1)
     lane_float = lane.astype(jnp.float32)
@@ -153,28 +266,73 @@
         key_mark_ref[at, :] = jnp.where(
             lane < blk_count, jnp.where(image_is[at], 0.0, 1.0), block_is
         ).astype(jnp.bfloat16)
-    wide, experts = slot_keys_wide_ref.shape[0], slot_keys_ref.shape[1]
+    wide, experts = slot_keys_wide_ref.shape[0], slot_keys_ref.shape[0]
     column = lax.broadcasted_iota(jnp.int32, (wide, experts), 0)
     expert = lax.broadcasted_iota(jnp.int32, (wide, experts), 1)
     spread = jnp.where(column // blk_count == expert, 1.0, 0.0).astype(jnp.bfloat16)
-    slot_keys_wide_ref[...] = dot(spread, slot_keys_ref[...], ((1,), (1,))).astype(jnp.bfloat16)
+    slot_keys_wide_ref[...] = dot(spread, slot_keys_ref[...]).astype(jnp.bfloat16)
 
     copies[0].wait()
-    place_block(own_ref[...].astype(jnp.float32), place, project_in_ref, ordered_ref, joint_ref)
-    place_arrived(near_ref, project_in_ref, ordered_ref, joint_ref, certain)
+    own_index, near_slot = (0, 1) if certain else (own_place, None)
+    place_block(own_ref[...].astype(jnp.float32), own_index, project_in_ref, ordered_ref, joint_ref)
+    near_place = place_arrived(near_ref, near_slot, project_in_ref, ordered_ref, joint_ref)
+    note_place(places_ref, 0, own_place)
+    note_place(places_ref, 1, near_place)
+    if certain:
+        places = (own_place, near_place)
+        attention = Attention(
+            joint_ref,
+            gathered(query_mark_ref, places, rows),
+            gathered(key_mark_ref, places, rows),
+        )
+        state = top_ref, picked_ref, total_ref
+        span = slice(0, 2 * rows)
+        tasks = []
+        for pair in range(ordered_ref.shape[1] // LANES):
+            kept = functools.partial(keep_state, state, pair, span)
+            tasks.append(attention.begin(kept, pair, 0, 2 * rows, 2 * rows))
+        staggered(tasks)
     copies[1].wait()
 
 
 def middle_kernel(*refs, certain):
-    *arrived, project_in_ref, _, _, ordered_ref, joint_ref = refs
-    for ref in arrived:
-        place_arrived(ref, project_in_ref, ordered_ref, joint_ref, certain)
+    *arrived, project_in_ref, query_mark_ref, key_mark_ref = refs[:-12]
+    ordered_ref, joint_ref, places_ref, *state = refs[-6:]
+    width = ordered_ref.shape[1]
+    for slot, ref in enumerate(arrived, start=2):
+        place = place_arrived(
+            ref, slot if certain else None, project_in_ref, ordered_ref, joint_ref
+        )
+        if not certain:
+            continue
+        rows = ordered_ref.shape[0] // (len(arrived) + 3)
+        note_place(places_ref, slot, place)
+        places = [read_place(places_ref, n) for n in range(slot)] + [place]
+        attention = Attention(
+            joint_ref,
+            gathered(query_mark_ref, places, rows),
+            gathered(key_mark_ref, places, rows),
+        )
+        stop = slot * rows
+        block = slice(stop, stop + rows)
+        span = slice(0, stop)
+        tasks = []
+        for pair in range(width // LANES):
+            kept, new = (functools.partial(keep_state, state, pair, at) for at in (span, block))
+            old = functools.partial(read_state, state, pair, span)
+            tasks.append(attention.extend(kept, pair, stop, block, old))
+            tasks.append(attention.begin(new, pair, stop, stop + rows, stop + rows))
+        staggered(tasks)
 
 
 def front_kernel(
     arrived_ref,
     _ordered_ref,
     _joint_ref,
+    places_ref,
+    top_ref,
+    picked_ref,
+    total_ref,
     image_ref,
     query_mark_ref,
     key_mark_ref,
@@ -191,51 +349,59 @@
     expert_in_ref,
     expert_out_ref,
     context_ref,
+    moe_normed_ref,
     sems,
     *,
     certain,
 ):
     tok_count, width = ordered_ref.shape
+    blk_count = slot_in_ref.shape[1]
+    rows = tok_count // blk_count
     copies = [
         pltpu.make_async_copy(expert_in_hbm, expert_in_ref, sems.at[0]),
         pltpu.make_async_copy(expert_out_hbm, expert_out_ref, sems.at[1]),
     ]
     for copy in copies:
         copy.start()
-    place_arrived(arrived_ref, project_in_ref, ordered_ref, joint_ref, certain)
-
-    lane = lax.broadcasted_iota(jnp.int32, (1, LANES), 1)
-    first = lane < HEAD
-    zero = jnp.zeros((), jnp.bfloat16)
-    ones = jnp.ones((tok_count, LANES), jnp.bfloat16)
-    scale = HEAD ** (-0.5) * math.log2(math.e)
+    last = blk_count - 1
+    place = place_arrived(
+        arrived_ref, last if certain else None, project_in_ref, ordered_ref, joint_ref
+    )
+    places = list(range(blk_count))
+    if certain:
+        places = [read_place(places_ref, n) for n in range(last)] + [place]
+    attention = Attention(
+        joint_ref,
+        gathered(query_mark_ref, places, rows),
+        gathered(key_mark_ref, places, rows),
+    )
+    state = top_ref, picked_ref, total_ref
+    stop = last * rows if certain else 0
+
+    def keep_context(pair, rows, tops, picked, total):
+        at = slice(pair * LANES, (pair + 1) * LANES)
+        context_ref[rows, at] = (picked / total).astype(jnp.bfloat16)
+
+    span, block = slice(0, stop), slice(stop, tok_count)
+    tasks = []
     for pair in range(width // LANES):
-        at = pair * LANES
-        query = joint_ref[:, at : at + LANES]
-        key = joint_ref[:, width + at : width + at + LANES]
-        value = joint_ref[:, 2 * width + at : 2 * width + at + LANES]
-        keys = jnp.concatenate([key, key_mark_ref[...]], axis=1)
-        values = jnp.concatenate([value, ones], axis=1)
-        parts = []
-        for keep in (first, ~first):
-            queries = jnp.concatenate(
-                [jnp.where(keep, query, zero), query_mark_ref[...]], axis=1
-            )
-            scores = dot(queries, keys, ((1,), (1,)))
-            top = jnp.max(scores, axis=1, keepdims=True)
-            raised = jnp.exp2((scores - top) * scale).astype(jnp.bfloat16)
-            parts.append(dot(raised, values))
-        picked = jnp.where(first, parts[0][:, :LANES], parts[1][:, :LANES])
-        total = jnp.where(first, parts[0][:, LANES:], parts[1][:, LANES:])
-        context_ref[:, at : at + LANES] = (picked / total).astype(jnp.bfloat16)
+        kept, new = (functools.partial(keep_context, pair, at) for at in (span, block))
+        if certain:
+            old = functools.partial(read_state, state, pair, span)
+            tasks.append(attention.extend(kept, pair, stop, block, old))
+        tasks.append(attention.begin(new, pair, stop, tok_count, tok_count))
+    staggered(tasks)
 
     hidden = (
         ordered_ref[...].astype(jnp.float32) + dot(context_ref[...], project_out_ref[...])
     ).astype(jnp.bfloat16)
-    hidden_ref[...] = hidden
-    moe_normed = layer_norm(hidden.astype(jnp.float32)).astype(jnp.bfloat16)
+    normed = layer_norm(hidden.astype(jnp.float32)).astype(jnp.bfloat16)
+    for slot, place in enumerate(places):
+        at = slice(slot * rows, (slot + 1) * rows)
+        hidden_ref[block_at(place, rows), :] = hidden[at]
+        moe_normed_ref[block_at(place, rows), :] = normed[at]
+    moe_normed = moe_normed_ref[...]
     logits = dot(slot_keys_ref[...], moe_normed, ((1,), (1,)))
-    blk_count = slot_in_ref.shape[1]
     column_image = lax.broadcasted_iota(jnp.int32, (logits.shape[0], 1), 0) % blk_count
     member = image_ref[...] == column_image
     top = jnp.max(jnp.where(member, logits, NEGATIVE), axis=1, keepdims=True)
@@ -336,14 +502,18 @@
             pltpu.VMEM((columns, width), jnp.bfloat16),
             pltpu.VMEM((tok_count, width), jnp.bfloat16),
             pltpu.VMEM((tok_count, 3 * width), jnp.bfloat16),
+            pltpu.VMEM((data_count, LANES), jnp.float32),
+            pltpu.VMEM((width // HEAD, tok_count, LANES), jnp.float32),
+            pltpu.VMEM((width // LANES, tok_count, LANES), jnp.float32),
+            pltpu.VMEM((width // LANES, tok_count, LANES), jnp.float32),
         ],
         in_specs=[whole(pltpu.SMEM)] * 2 + [whole()] * 4 + [whole(pltpu.HBM)] * 2,
-        out_specs=[whole()] * 8,
+        out_specs=[whole()] * 12,
         scratch_shapes=[pltpu.SemaphoreType.DMA((2,))],
         compiler_params=params,
         name="prepare",
     )(
-        *resident(owner_slot, block_mask, segment, slot_keys, memory_space=pltpu.HBM),
+        *resident(owner_slot, block_mask, segment, slot_keys.T, memory_space=pltpu.HBM),
         *resident(own, near),
         *resident(project_in, project_out, memory_space=pltpu.HBM),
     )
@@ -352,30 +522,31 @@
     placed_shapes = tuple(pltpu.VMEM(array.shape, array.dtype) for array in placed)
     *earlier, last = far
     if earlier:
-        base = len(earlier) + 1
+        base = len(earlier) + 3
         placed = pl.pallas_call(
             functools.partial(middle_kernel, certain=certain),
             out_shape=placed_shapes,
-            in_specs=[whole()] * (base + 2),
-            out_specs=(whole(),) * 2,
-            input_output_aliases={base + n: n for n in range(2)},
+            in_specs=[whole()] * (base + len(placed)),
+            out_specs=(whole(),) * len(placed),
+            input_output_aliases={base + n: n for n in range(len(placed))},
             compiler_params=params,
             name="middle",
-        )(*resident(*earlier, project_in, *placed))
+        )(*resident(*earlier, project_in, query_mark, key_mark, *placed))
     *_, hidden, slot_in, combine, expert_in, expert_out = pl.pallas_call(
         functools.partial(front_kernel, certain=certain),
         out_shape=(
-            *placed_shapes,
+            *placed_shapes[:2],
             pltpu.VMEM((tok_count, width), jnp.bfloat16),
             pltpu.VMEM((expert_count, blk_count, width), jnp.bfloat16),
             pltpu.VMEM((tok_count, columns), jnp.bfloat16),
             pltpu.VMEM(expert_in.shape, jnp.bfloat16),
             pltpu.VMEM(expert_out.shape, jnp.bfloat16),
         ),
-        in_specs=[whole()] * 9 + [whole(pltpu.HBM)] * 2,
+        in_specs=[whole()] * 13 + [whole(pltpu.HBM)] * 2,
         out_specs=(whole(),) * 7,
         input_output_aliases={1 + n: n for n in range(2)},
         scratch_shapes=[
+            pltpu.VMEM((tok_count, width), jnp.bfloat16),
             pltpu.VMEM((tok_count, width), jnp.bfloat16),
             pltpu.SemaphoreType.DMA((2,)),
         ],

time: 49.3 us -> 50.9 us (1.032)
  Pallas kernels: 16.4 us -> 20.8 us
  local copies, waits for them, and re-layouts: 1.61 us -> 0 us
  waiting for transfers between devices: 2.62 us -> 1.42 us
    pallas_call x1, Pallas kernels: 0.82 us -> 2.8 us  [per_device(): pl.pallas_call(functools.partial(middle_kernel, certain=certain), out_sha...]
    unnamed x1 -> x0, local copies, waits for them, and re-layouts: 1.61 us -> none
    pallas_call x1, Pallas kernels: 6.85 us -> 8.45 us  [per_device(): pl.pallas_call(functools.partial(front_kernel, certain=certain), out_shap...]
    ppermute x3, waiting for transfers between devices: 2.62 us -> 1.42 us  [per_device(): lax.ppermute(send, 'dp', [(i, i ^ flip) for i in range(data_count)])]
    pallas_call x1, Pallas kernels: 4.41 us -> 5.26 us  [per_device(): pl.pallas_call(functools.partial(prepare_kernel, columns=column_count, ce...]
  transfers between devices with their start and end apart: 3 -> 3, of which waited for: 1 -> 2; matrix products, arithmetic and copies ran while one was open for 3% -> 0% of each run, Pallas kernels for 11% -> 16%
where the time goes in v6:
time: 50.9 us; the launch traced here: 50.7 us
  blocking collectives  25.2 us (50%)
  Pallas kernels  20.8 us (41%)
  starting transfers between devices  3.18 us (6%)
  waiting for transfers between devices  1.42 us (3%)
    all_to_all x1, blocking collectives, per_device(): lax.all_to_all(slot_in, AXES, split_axis=0, concat_axis=0, tiled=True)  13.9 us
    all_to_all x1, blocking collectives, per_device(): lax.all_to_all(produced, AXES, split_axis=0, concat_axis=0, tiled=True)  11.4 us
    pallas_call x1, Pallas kernels, per_device(): pl.pallas_call(functools.partial(front_kernel, certain=certain), out_shap...  8.45 us
    pallas_call x1, Pallas kernels, per_device(): pl.pallas_call(functools.partial(prepare_kernel, columns=column_count, ce...  5.26 us
    ppermute x3, starting transfers between devices, per_device(): lax.ppermute(send, 'dp', [(i, i ^ flip) for i in range(data_count)])  3.18 us
    pallas_call x1, Pallas kernels, per_device(): pl.pallas_call(functools.partial(middle_kernel, certain=certain), out_sha...  2.8 us
    pallas_call x1, Pallas kernels, per_device(): pl.pallas_call(expert_kernel, out_shape=pltpu.VMEM(slots_here.shape, jnp....  1.89 us
    ppermute x3, waiting for transfers between devices, per_device(): lax.ppermute(send, 'dp', [(i, i ^ flip) for i in range(data_count)])  1.42 us
  transfers between devices with their start and end apart: 3, of which 2 were waited for; matrix products, arithmetic and copies ran while one was open for 0% of the time, Pallas kernels for 16%

profile of v6, /device:TPU:0, one launch (start us, length us, event | category | flops | bytes accessed | tf_op | source)
XLA Modules:
  0.0 50.7 jit_solution(6806097785575526808)
XLA Ops:
  0.0 1.3 %send.1 = (bf16[97,8,128]{2,1,0:T(8,128)(2,1)S(1)}, bf16[97,8,128]{2,1,0:T(8,128)(2,1)S(1)}, bf16[97,8,128]{2,1,0:T(8,128)(2,1)S(1)}, bf16[128,768]{1,0:T(8,128)(2,1)S(1)}) custom-call(s32[4]{0:T(128)} %owner_ref.3, bf16[512,768]{1,0:T(8,128)(2,1)} %patches_ref.1), custom_call_target="tpu_custom_call" | custom-call | tf_op jit(solution)/shard_map/send/pallas_call | solution.py:479
  1.3 0.6 %collective-permute-start.2 = (bf16[97,8,128]{2,1,0:T(8,128)(2,1)S(1)}, bf16[97,8,128]{2,1,0:T(8,128)(2,1)S(1)}, u32[]{:S(2)}, u32[]{:S(2)}) collective-permute-start(bf16[97,8,128]{2,1,0:T(8,128)(2,1)S(1)} %get-tuple-element.35), channel_id=1, source_target_pairs={{0,8},{8,0},{16,24},{24,16},{1,9},{9,1},{17,25},{25,17},{2,10},{10... | collective-permute-start | bytes 595976 | tf_op jit(solution)/shard_map/ppermute | solution.py:490
  1.8 2.6 %collective-permute-start.1 = (bf16[97,8,128]{2,1,0:T(8,128)(2,1)S(1)}, bf16[97,8,128]{2,1,0:T(8,128)(2,1)S(1)}, u32[]{:S(2)}, u32[]{:S(2)}) collective-permute-start(bf16[97,8,128]{2,1,0:T(8,128)(2,1)S(1)} %get-tuple-element.33), channel_id=1, source_target_pairs={{0,16},{8,24},{16,0},{24,8},{1,17},{9,25},{17,1},{25,9},{2,18},{10... | collective-permute-start | bytes 595976 | tf_op jit(solution)/shard_map/ppermute | solution.py:490
  4.4 0.0 collective-permute-start
  4.5 0.0 collective-permute-done.2.near_ref
  4.5 5.3 %prepare.1 = (bf16[768,2304]{1,0:T(8,128)(2,1)S(1)}, bf16[768,768]{1,0:T(8,128)(2,1)S(1)}, s32[1,512]{1,0:T(1,128)S(1)}, bf16[512,128]{1,0:T(8,128)(2,1)S(1)}, b...) custom-call(s32[4]{0:T(128)} %owner_ref.3, ...), custom_call_target="tpu_custom_call" | custom-call | tf_op jit(solution)/shard_map/prepare/pallas_call | solution.py:494
  9.7 0.5 collective-permute-done.1.refs_0_
  10.2 2.8 %middle.1 = (bf16[512,768]{1,0:T(8,128)(2,1)S(1)}, bf16[512,2304]{1,0:T(8,128)(2,1)S(1)}, f32[4,128]{1,0:T(4,128)S(1)}, f32[12,512,128]{2,1,0:T(8,128)S(1)}, f32...) custom-call(bf16[97,8,128]{2,1,0:T(8,128)(2,1)S(1)} %collective-perm, ...), custom_call_target="tpu_custom_call", output_to_operand_aliasing={{0}: (4, {}), {1}: (5, {}), {2}: (6, {}), {3}: (7, {}), {4}... | custom-call | tf_op jit(solution)/shard_map/middle/pallas_call | solution.py:526
  13.0 0.9 %collective-permute-done.arrived_ref = bf16[97,8,128]{2,1,0:T(8,128)(2,1)S(1)} collective-permute-done((bf16[97,8,128]{2,1,0:T(8,128)(2,1)S(1)}, bf16[97,8,128]{2,1,0:T(8,128)(2,1)S(1)}, u32[]{:S(2)}, u32[]{:S(2)}) %collective-permute-start) | collective-permute-done | bytes 198688 | tf_op jit(solution)/shard_map/ppermute | solution.py:490
  13.9 8.4 %front.1 = (bf16[512,768]{1,0:T(8,128)(2,1)S(1)}, bf16[512,2304]{1,0:T(8,128)(2,1)S(1)}, bf16[512,768]{1,0:T(8,128)(2,1)S(1)}, bf16[32,4,768]{2,1,0:T(4,128)(2,1...) custom-call(bf16[97,8,128]{2,1,0:T(8,128)(2,1)S(1)} %collective-perm, ...), custom_call_target="tpu_custom_call", output_to_operand_aliasing={{0}: (1, {}), {1}: (2, {})} | custom-call | tf_op jit(solution)/shard_map/front/pallas_call | solution.py:535
  22.4 13.9 %all_to_all.10.arrived_ref = bf16[32,4,768]{2,1,0:T(4,128)(2,1)S(1)} all-to-all(bf16[32,4,768]{2,1,0:T(4,128)(2,1)S(1)} %get-tuple-element.56), channel_id=1, replica_groups=mesh['dp'=4,'expert'=8] {'dp','expert'}, dimensions={0} | all-to-all | bytes 393216 | tf_op jit(solution)/shard_map/all_to_all | solution.py:560
  36.3 1.9 %expert.1 = bf16[32,4,768]{2,1,0:T(4,128)(2,1)S(1)} custom-call(bf16[32,4,768]{2,1,0:T(4,128)(2,1)S(1)} %all_to_all.10.arrived_ref, bf16[1,768,3072]{2,1,0:T(8,128)(2,1)S(1)} %get-tuple-element.57.expert_in_ref, bf16[1,3072,768]{2,1,0:T(8,128)(2,1)S(1)} %get-tuple-element.58.expert_out_ref), custom_call_target="tpu_custom_call" | custom-call | tf_op jit(solution)/shard_map/expert/pallas_call | solution.py:561
  38.2 11.4 %all_to_all.11.returned_ref = bf16[32,4,768]{2,1,0:T(4,128)(2,1)S(1)} all-to-all(bf16[32,4,768]{2,1,0:T(4,128)(2,1)S(1)} %expert.1), channel_id=1, replica_groups=mesh['dp'=4,'expert'=8] {'dp','expert'}, dimensions={0} | all-to-all | bytes 393216 | tf_op jit(solution)/shard_map/all_to_all | solution.py:570
  49.5 1.1 %combine.1 = bf16[512,768]{1,0:T(8,128)(2,1)} custom-call(bf16[512,768]{1,0:T(8,128)(2,1)S(1)} %get-tuple-element.54.hidden_ref, bf16[512,128]{1,0:T(8,128)(2,1)S(1)} %get-tuple-element.55.combine_ref, bf16[32,4,768]{2,1,0:T(4,128)(2,1)S(1)} %all_to_all.11.returned_ref), custom_call_target="tpu_custom_call" | custom-call | tf_op jit(solution)/shard_map/combine/pallas_call | solution.py:571
Async XLA Ops:
  1.3 3.2 %collective-permute-start.2 = (bf16[97,8,128]{2,1,0:T(8,128)(2,1)S(1)}, bf16[97,8,128]{2,1,0:T(8,128)(2,1)S(1)}, u32[]{:S(2)}, u32[]{:S(2)}) collective-permute-start(bf16[97,8,128]{2,1,0:T(8,128)(2,1)S(1)} %get-tuple-element.35), channel_id=1, source_target_pairs={{0,8},{8,0},{16,24},{24,16},{1,9},{9,1},{17,25},{25,17},{2,10},{10... | collective-permute-start | bytes 595976 | tf_op jit(solution)/shard_map/ppermute | solution.py:490
  1.8 8.4 %collective-permute-start.1 = (bf16[97,8,128]{2,1,0:T(8,128)(2,1)S(1)}, bf16[97,8,128]{2,1,0:T(8,128)(2,1)S(1)}, u32[]{:S(2)}, u32[]{:S(2)}) collective-permute-start(bf16[97,8,128]{2,1,0:T(8,128)(2,1)S(1)} %get-tuple-element.33), channel_id=1, source_target_pairs={{0,16},{8,24},{16,0},{24,8},{1,17},{9,25},{17,1},{25,9},{2,18},{10... | collective-permute-start | bytes 595976 | tf_op jit(solution)/shard_map/ppermute | solution.py:490
  4.4 9.5 %collective-permute-start = (bf16[97,8,128]{2,1,0:T(8,128)(2,1)S(1)}, bf16[97,8,128]{2,1,0:T(8,128)(2,1)S(1)}, u32[]{:S(2)}, u32[]{:S(2)}) collective-permute-start(bf16[97,8,128]{2,1,0:T(8,128)(2,1)S(1)} %get-tuple-element.32), channel_id=1, source_target_pairs={{0,24},{8,16},{16,8},{24,0},{1,25},{9,17},{17,9},{25,1},{2,26},{10... | collective-permute-start | bytes 595976 | tf_op jit(solution)/shard_map/ppermute | solution.py:490
